TPU v7x, 256 devices: a whole 4x4x8 slice. The times are simulated.
256 devices in a mesh: dp: 32 (over y_lo, z, core), ctx: 8 (over y_hi, x).
Axes of the slice: x: 4, y: 4 (y_hi: 2, y_lo: 2; y = y_hi * 2 + y_lo), z: 8, core: 2. Of those that a mesh axis runs over, the one named last changes fastest.
Arguments:
- query_proj: bfloat16 [64, 512, 4096], P('dp', 'ctx'), may hold values from -5 to 5
- key_proj: bfloat16 [64, 512, 1024], P('dp', 'ctx'), may hold values from -5 to 5
- value_proj: bfloat16 [64, 512, 1024], P('dp', 'ctx'), may hold values from -6 to 6
- grad_attn: bfloat16 [64, 512, 4096], P('dp', 'ctx'), may hold values from -6 to 6
- doc_lengths: int32 [64, 8], replicated, may hold values from 1 to 128, 512 in all within a row
- mask_tiles: int32 [64, 8, 8], replicated, may hold values from 0 to 1, as said below
- pair_flags: int32 [32], replicated, may hold values from 0 to 1, as said below
Outputs:
- attn_out: bfloat16 [64, 512, 4096], P('dp', 'ctx')
- grad_query: bfloat16 [64, 512, 4096], P('dp', 'ctx')
- grad_key: bfloat16 [64, 512, 1024], P('dp', 'ctx')
- grad_value: bfloat16 [64, 512, 1024], P('dp', 'ctx')
Inputs may be any that keep to these rules, and one draw needn't show every extreme that they name: `doc_lengths`: each row sums to 512. mask_tiles[n, t, t] = 1 for every sequence n and tile t. pair_flags[r] = pair_flags[r XOR (16)] for every r.
All inputs are finite; a program needn't handle non-finite values.
Results may differ from a plain program's by a relative error of at most 0.03.
Values may be sent and summed in bfloat16 or wider, within the bound.
A program may use at most 128 MiB of HBM per device.

v0:
```python
import jax
import jax.numpy as jnp
from jax import lax
from jax.sharding import PartitionSpec as P

QUERY_HEADS = 32
KEY_VALUE_HEADS = 8
HEAD_SIZE = 128


def from_partner(value, axis, distance):
    mask = 2**distance
    pairs = [(source, source ^ mask) for source in range(lax.axis_size(axis))]
    return lax.ppermute(value, axis, pairs)


def sequence_core(
    query_rows, sequence_keys, sequence_values, sequence_gradients, lengths, tile_table, row_start
):
    rows = query_rows.shape[0]
    length_total = sequence_keys.shape[0]
    groups = sequence_keys.shape[1] // HEAD_SIZE
    group_ratio = QUERY_HEADS // KEY_VALUE_HEADS
    scale = HEAD_SIZE ** (-0.5)
    row_pos = row_start + jnp.arange(rows, dtype=jnp.int32)
    col_pos = jnp.arange(length_total, dtype=jnp.int32)
    ends = jnp.cumsum(lengths)[:-1]
    row_doc = jnp.sum((row_pos[:, None] >= ends[None, :]).astype(jnp.int32), axis=1)
    col_doc = jnp.sum((col_pos[:, None] >= ends[None, :]).astype(jnp.int32), axis=1)
    tile_count = tile_table.shape[0]
    tile_len = length_total // tile_count
    tile_ids = jnp.arange(tile_count, dtype=jnp.int32)
    row_pick = ((row_pos // tile_len)[:, None] == tile_ids[None, :]).astype(jnp.float32)
    col_pick = ((col_pos // tile_len)[:, None] == tile_ids[None, :]).astype(jnp.float32)
    tile_map = jnp.dot(jnp.dot(row_pick, tile_table.astype(jnp.float32)), col_pick.T) > 0.5
    allowed = (
        (col_pos[None, :] <= row_pos[:, None])
        & ((col_doc[None, :] == row_doc[:, None]) | (col_doc[None, :] == 0))
        & tile_map
    )
    heads_of_queries = query_rows.reshape(rows, groups, group_ratio, HEAD_SIZE)
    heads_of_keys = sequence_keys.reshape(length_total, groups, HEAD_SIZE)
    heads_of_values = sequence_values.reshape(length_total, groups, HEAD_SIZE)
    head_gradients = sequence_gradients.reshape(rows, groups, group_ratio, HEAD_SIZE)
    scores = (
        jnp.einsum(
            "igrd,jgd->grij", heads_of_queries, heads_of_keys, preferred_element_type=jnp.float32
        )
        * scale
    )
    scores = jnp.where(allowed, scores, -1e30)
    peak = jnp.max(scores, axis=-1, keepdims=True)
    expd = jnp.where(allowed, jnp.exp(scores - peak), 0.0)
    probs = expd / jnp.sum(expd, axis=-1, keepdims=True)
    probs_b = probs.astype(jnp.bfloat16)
    attn = jnp.einsum(
        "grij,jgd->igrd", probs_b, heads_of_values, preferred_element_type=jnp.float32
    ).astype(jnp.bfloat16)
    delta = jnp.transpose(
        jnp.sum(head_gradients.astype(jnp.float32) * attn.astype(jnp.float32), axis=-1), (1, 2, 0)
    )
    value_gradient = jnp.einsum(
        "grij,igrd->jgd", probs_b, head_gradients, preferred_element_type=jnp.float32
    )
    dprobs = jnp.einsum(
        "igrd,jgd->grij", head_gradients, heads_of_values, preferred_element_type=jnp.float32
    )
    dscores = (probs * (dprobs - delta[..., None]) * scale).astype(jnp.bfloat16)
    grad_q = jnp.einsum(
        "grij,jgd->igrd", dscores, heads_of_keys, preferred_element_type=jnp.float32
    )
    key_gradient = jnp.einsum(
        "grij,igrd->jgd", dscores, heads_of_queries, preferred_element_type=jnp.float32
    )
    return (
        attn.reshape(rows, -1),
        grad_q.astype(jnp.bfloat16).reshape(rows, -1),
        key_gradient.reshape(length_total, -1),
        value_gradient.reshape(length_total, -1),
    )


def attend(query_rows, keys_in, values_in, grads_in, lengths_all, tiles_all, first_id, second_id):
    seq_ids = jnp.stack([first_id, second_id])
    lengths_pair = jnp.take(lengths_all, seq_ids, axis=0)
    tiles_pair = jnp.take(tiles_all, seq_ids, axis=0)
    ctx_rank = lax.axis_index("ctx")
    seq_dev = query_rows.shape[1]
    keys_all, values_all = (
        lax.all_gather(keys_in, "ctx", axis=1, tiled=True),
        lax.all_gather(values_in, "ctx", axis=1, tiled=True),
    )
    pieces = [
        sequence_core(
            query_rows[seq_slot],
            keys_all[seq_slot],
            values_all[seq_slot],
            grads_in[seq_slot],
            lengths_pair[seq_slot],
            tiles_pair[seq_slot],
            ctx_rank * seq_dev,
        )
        for seq_slot in range(2)
    ]
    attn = jnp.stack([pieces[0][0], pieces[1][0]])
    grad_q = jnp.stack([pieces[0][1], pieces[1][1]])
    key_terms = jnp.stack([pieces[0][2], pieces[1][2]])
    value_terms = jnp.stack([pieces[0][3], pieces[1][3]])
    key_sums, value_sums = (
        lax.psum_scatter(key_terms, "ctx", scatter_dimension=1, tiled=True),
        lax.psum_scatter(value_terms, "ctx", scatter_dimension=1, tiled=True),
    )
    return (attn, grad_q, key_sums.astype(jnp.bfloat16), value_sums.astype(jnp.bfloat16))


def take_second(mine, arrived, swapped):
    return jnp.stack([mine[0], jnp.where(swapped, arrived, mine[1])])


def shards(query_proj, key_proj, value_proj, grad_attn, doc_lengths, mask_tiles, pair_flags):
    dp_size = lax.axis_size("dp")
    dp_rank = lax.axis_index("dp")
    far_bit = dp_size.bit_length() - 2
    partner = jnp.bitwise_xor(dp_rank, dp_size // 2)
    pair_flag = lax.dynamic_index_in_dim(pair_flags, dp_rank, 0, keepdims=False)
    swapped = pair_flag == 1
    first_id = 2 * dp_rank
    second_id = jnp.where(swapped, 2 * partner + 1, 2 * dp_rank + 1)
    arrived = from_partner((query_proj[1], key_proj[1], value_proj[1], grad_attn[1]), "dp", far_bit)
    query_now = take_second(query_proj, arrived[0], swapped)
    key_now = take_second(key_proj, arrived[1], swapped)
    value_now = take_second(value_proj, arrived[2], swapped)
    grad_now = take_second(grad_attn, arrived[3], swapped)
    return attend(
        query_now, key_now, value_now, grad_now, doc_lengths, mask_tiles, first_id, second_id
    )


def solution(mesh):
    in_specs = (
        P("dp", "ctx", None),
        P("dp", "ctx", None),
        P("dp", "ctx", None),
        P("dp", "ctx", None),
        P(),
        P(),
        P(),
    )
    out_specs = (
        P("dp", "ctx", None),
        P("dp", "ctx", None),
        P("dp", "ctx", None),
        P("dp", "ctx", None),
    )
    return jax.shard_map(shards, mesh=mesh, in_specs=in_specs, out_specs=out_specs, check_vma=False)
```

profile of v0, /device:TPU:64, one launch (start us, length us, event | category | flops | bytes accessed | tf_op | source)
XLA Modules:
  0.0 378.6 jit_solution(14901232772893351566)
XLA Ops:
  8.3 1.7 collective-permute-start.1
  11.5 1.2 dynamic_slice.4
  14.0 2.4 collective-permute-done
  18.5 2.2 fusion.67
  20.7 1.6 collective-permute-start.2
  25.7 1.5 gather_fusion.1
  27.2 1.2 reshape_squeeze_stack_squeeze.6
  28.4 1.2 reshape_squeeze_stack_squeeze.7
  31.9 4.0 %collective-permute-done.2 = bf16[64,4096]{1,0:T(8,128)(2,1)} collective-permute-done((bf16[64,4096]{1,0:T(8,128)(2,1)}, bf16[64,4096]{1,0:T(8,128)(2,1)}, u32[]{:S(2)}, u32[]{:S(2)}) %collective-permute-start.2) | collective-permute-done | bytes 524320 | tf_op jit(solution)/shard_map/ppermute | solution.py:14
  35.9 1.2 reshape_squeeze_stack.6
  37.1 10.8 %collective-permute-done.3 = bf16[64,4096]{1,0:T(8,128)(2,1)} collective-permute-done((bf16[64,4096]{1,0:T(8,128)(2,1)}, bf16[64,4096]{1,0:T(8,128)(2,1)}, u32[]{:S(2)}, u32[]{:S(2)}) %collective-permute-start.3) | collective-permute-done | bytes 524320 | tf_op jit(solution)/shard_map/ppermute | solution.py:14
  48.0 1.1 reshape_squeeze_stack.7
  49.2 33.8 %all-gather.3.cloned.1.call-done = bf16[2,512,1024]{2,0,1:T(2,128)(2,1)} async-done(((bf16[2,64,1024]{2,0,1:T(2,128)(2,1)}), bf16[2,512,1024]{2,0,1:T(2,128)(2,1)}) %all-gather.3.cloned.1.call-update) | async-done | bytes 2097168 | tf_op jit(solution)/shard_map/all_gather | solution.py:91
  83.0 6.6 %fusion.65 = (bf16[1,512,1024]{2,0,1:T(2,128)(2,1)}, bf16[1,512,1024]{2,0,1:T(2,128)(2,1)S(1)}) fusion(bf16[2,512,1024]{2,0,1:T(2,128)(2,1)} %all-gather.3.cloned.1.call-done), kind=kLoop, calls=%fused_computation.121 | loop fusion | bytes 4194304 | tf_op jit(solution)/shard_map/slice | solution.py:97
  89.5 5.8 %copy.180 = bf16[1,512,1024]{1,2,0:T(8,128)(2,1)} copy(bf16[1,512,1024]{2,0,1:T(2,128)(2,1)} %get-tuple-element.8) | data formatting | bytes 2097152
  95.3 4.2 %copy.182 = bf16[1,512,1024]{1,2,0:T(8,128)(2,1)} copy(bf16[1,512,1024]{2,0,1:T(2,128)(2,1)S(1)} %get-tuple-element.9) | data formatting | bytes 2097152
  99.6 45.6 %all-gather.5.cloned.1.call-done = bf16[2,512,1024]{2,0,1:T(2,128)(2,1)} async-done(((bf16[2,64,1024]{2,0,1:T(2,128)(2,1)}), bf16[2,512,1024]{2,0,1:T(2,128)(2,1)}) %all-gather.5.cloned.1.call-update) | async-done | bytes 2097168 | tf_op jit(solution)/shard_map/all_gather | solution.py:90
  145.1 6.5 %fusion.64 = (bf16[1,512,1024]{2,0,1:T(2,128)(2,1)S(1)}, bf16[1,512,1024]{2,0,1:T(2,128)(2,1)}) fusion(bf16[2,512,1024]{2,0,1:T(2,128)(2,1)} %all-gather.5.cloned.1.call-done), kind=kLoop, calls=%fused_computation.120 | loop fusion | bytes 4194304 | tf_op jit(solution)/shard_map/slice | solution.py:96
  151.6 2.6 copy.181
  154.2 4.6 %copy.183 = bf16[1,512,1024]{1,2,0:T(8,128)(2,1)S(1)} copy(bf16[1,512,1024]{2,0,1:T(2,128)(2,1)} %get-tuple-element.7) | data formatting | bytes 2097152
  158.8 1.7 fusion.30
  160.5 2.1 fusion.70
  164.2 1.5 multiply_reduce_fusion
  165.7 1.1 fusion.4
  166.8 2.0 fusion.28
  168.8 2.9 copy.147
  172.4 2.1 fusion.71
  176.1 1.5 multiply_reduce_fusion.1
  177.6 1.1 fusion.7
  178.7 2.1 fusion.32
  180.8 2.9 copy.146
  183.7 4.7 %pad_maximum_fusion = f32[2,512,1024]{2,1,0:T(8,128)} fusion(f32[1,512,1024]{2,1,0:T(8,128)} %copy.147, f32[1,512,1024]{2,1,0:T(8,128)} %copy.146), kind=kLoop, calls=%fused_computation.4 | loop fusion | flops 1048576 | bytes 8388608 | tf_op jit(solution)/shard_map/stack | solution.py:107
  189.5 3.5 fusion.36
  193.0 2.9 copy.151
  195.9 3.5 fusion.39
  199.4 2.9 copy.150
  202.3 4.8 %pad_maximum_fusion.1 = f32[2,512,1024]{2,1,0:T(8,128)} fusion(f32[1,512,1024]{2,1,0:T(8,128)} %copy.151, f32[1,512,1024]{2,1,0:T(8,128)} %copy.150), kind=kLoop, calls=%fused_computation.5 | loop fusion | flops 1048576 | bytes 8388608 | tf_op jit(solution)/shard_map/stack | solution.py:108
  207.1 2.3 fusion.21
  209.4 1.2 copy.143
  210.6 2.3 stack_reshape.27
  212.9 2.3 copy.133
  215.1 2.3 stack_reshape.25
  219.0 1.5 copy.127
  220.8 1.1 pad_maximum_fusion.3
  223.0 54.5 %reduce-scatter.3.cloned.1.call-done = f32[2,64,1024]{2,1,0:T(8,128)} async-done(((f32[2,512,1024]{2,1,0:T(8,128)}), f32[2,64,1024]{2,1,0:T(8,128)}) %reduce-scatter.3.cloned.1.call-update) | async-done | bytes 524304 | tf_op jit(solution)/shard_map/reduce_scatter | solution.py:110
  277.5 1.8 convert_element_type.106
  279.2 91.1 %reduce-scatter.5.cloned.1.call-done = f32[2,64,1024]{2,1,0:T(8,128)} async-done(((f32[2,512,1024]{2,1,0:T(8,128)}), f32[2,64,1024]{2,1,0:T(8,128)}) %reduce-scatter.5.cloned.1.call-update) | async-done | bytes 524304 | tf_op jit(solution)/shard_map/reduce_scatter | solution.py:111
  370.3 1.8 convert_element_type.107
  (86 shorter events, 18.9 us)
Async XLA Ops:
  7.2 15.1 %copy-start.8 = (bf16[2,64,4096]{2,1,0:T(8,128)(2,1)S(1)}, bf16[2,64,4096]{2,1,0:T(8,128)(2,1)}, u32[]{:S(2)}) copy-start(bf16[2,64,4096]{2,1,0:T(8,128)(2,1)} %param.10) | copy-start | bytes 3145732
  7.2 16.4 %copy-start.17 = (s32[64,8]{0,1:T(8,128)S(1)}, s32[64,8]{0,1:T(8,128)}, u32[]{:S(2)}) copy-start(s32[64,8]{0,1:T(8,128)} %param.11) | copy-start | bytes 6148
  7.2 17.7 %copy-start.16 = (s32[64,8,8]{0,2,1:T(8,128)S(1)}, s32[64,8,8]{0,2,1:T(8,128)}, u32[]{:S(2)}) copy-start(s32[64,8,8]{0,2,1:T(8,128)} %param.12) | copy-start | bytes 49156
  7.2 75.8 %all-gather.3.cloned.1.call-start = ((), (), s32[]{:S(2)}) async-start(), calls=%async_computation.2 | async-start | bytes 2359296 | tf_op jit(solution)/shard_map/all_gather | solution.py:91
  8.3 5.7 %collective-permute-start.1 = (bf16[64,1024]{1,0:T(8,128)(2,1)S(1)}, bf16[64,1024]{1,0:T(8,128)(2,1)S(1)}, u32[]{:S(2)}, u32[]{:S(2)}) collective-permute-start(bf16[64,1024]{1,0:T(8,128)(2,1)S(1)} %get-tuple-element.15), channel_id=1, source_target_pairs={{0,128},{8,136},{16,144},{24,152},{32,160},{40,168},{48,176},{56,1... | collective-permute-start | bytes 393224 | tf_op jit(solution)/shard_map/ppermute | solution.py:14
  11.0 5.5 %collective-permute-start = (bf16[64,1024]{1,0:T(8,128)(2,1)S(1)}, bf16[64,1024]{1,0:T(8,128)(2,1)S(1)}, u32[]{:S(2)}, u32[]{:S(2)}) collective-permute-start(bf16[64,1024]{1,0:T(8,128)(2,1)S(1)} %get-tuple-element.17), channel_id=1, source_target_pairs={{0,128},{8,136},{16,144},{24,152},{32,160},{40,168},{48,176},{56,1... | collective-permute-start | bytes 393224 | tf_op jit(solution)/shard_map/ppermute | solution.py:14
  18.5 17.4 %copy-start.7 = (bf16[2,64,4096]{2,1,0:T(8,128)(2,1)S(1)}, bf16[2,64,4096]{2,1,0:T(8,128)(2,1)}, u32[]{:S(2)}) copy-start(bf16[2,64,4096]{2,1,0:T(8,128)(2,1)} %param.7) | copy-start | bytes 3145732
  18.5 126.6 %all-gather.5.cloned.1.call-start = ((), (), s32[]{:S(2)}) async-start(), calls=%async_computation.3 | async-start | bytes 2359296 | tf_op jit(solution)/shard_map/all_gather | solution.py:90
  20.7 15.2 %collective-permute-start.2 = (bf16[64,4096]{1,0:T(8,128)(2,1)}, bf16[64,4096]{1,0:T(8,128)(2,1)}, u32[]{:S(2)}, u32[]{:S(2)}) collective-permute-start(bf16[64,4096]{1,0:T(8,128)(2,1)} %get-tuple-element.13), channel_id=1, source_target_pairs={{0,128},{8,136},{16,144},{24,152},{32,160},{40,168},{48,176},{56,1... | collective-permute-start | bytes 1572872 | tf_op jit(solution)/shard_map/ppermute | solution.py:14
  23.1 24.8 %collective-permute-start.3 = (bf16[64,4096]{1,0:T(8,128)(2,1)}, bf16[64,4096]{1,0:T(8,128)(2,1)}, u32[]{:S(2)}, u32[]{:S(2)}) collective-permute-start(bf16[64,4096]{1,0:T(8,128)(2,1)} %get-tuple-element.11), channel_id=1, source_target_pairs={{0,128},{8,136},{16,144},{24,152},{32,160},{40,168},{48,176},{56,1... | collective-permute-start | bytes 1572872 | tf_op jit(solution)/shard_map/ppermute | solution.py:14
  30.8 246.7 %reduce-scatter.3.cloned.1.call-start = ((), (), s32[]{:S(2)}) async-start(), calls=%async_computation.4 | async-start | bytes 4718592 | tf_op jit(solution)/shard_map/reduce_scatter | solution.py:110
  162.7 1.0 copy-start.10
  162.7 1.5 copy-start.15
  163.0 3.8 copy-start
  165.7 1.1 copy-start.6
  166.8 2.0 copy-start.2
  166.8 4.9 %copy-start.5 = (bf16[64,8,4,128]{3,2,1,0:T(4,128)(2,1)S(1)}, bf16[64,8,4,128]{3,2,1,0:T(4,128)(2,1)}, u32[]{:S(2)}) copy-start(bf16[64,8,4,128]{3,2,1,0:T(4,128)(2,1)} %reshape_squeeze_stack_squeeze.6) | copy-start | bytes 1572868
  174.6 1.0 copy-start.9
  174.6 1.5 copy-start.14
  175.0 3.8 copy-start.1
  178.7 2.1 copy-start.3
  188.4 1.0 copy-start.11
  188.5 181.8 %reduce-scatter.5.cloned.1.call-start = ((), (), s32[]{:S(2)}) async-start(), calls=%async_computation.5 | async-start | bytes 4718592 | tf_op jit(solution)/shard_map/reduce_scatter | solution.py:111
  209.4 8.0 %copy-start.4 = (bf16[8,4,64,512]{3,2,1,0:T(8,128)(2,1)S(1)}, bf16[8,4,64,512]{3,2,1,0:T(8,128)(2,1)}, u32[]{:S(2)}) copy-start(bf16[8,4,64,512]{3,2,1,0:T(8,128)(2,1)} %copy-done.3) | copy-start | bytes 6291460
  218.1 2.7 copy-start.12
  218.1 3.7 copy-start.13
Sparse Core Ops, SparseCore 0:
  18.6 64.3 all-gather.2
  86.2 58.9 all-gather.4
  188.6 88.8 reduce-scatter.2
  281.5 88.7 reduce-scatter.4
where the time goes:
time: 380 us; the launch traced here: 379 us
  waiting for transfers between devices  243 us (64%)
  local copies, waits for them, and re-layouts  71.7 us (19%)
  matrix products  22.5 us (6%)
  other arithmetic  22.4 us (6%)
  between operations  14.8 us (4%)
  starting transfers between devices  4.39 us (1%)
    reduce_scatter x1, waiting for transfers between devices, attend(): lax.psum_scatter(value_terms, 'ctx', scatter_dimension=1, tiled=True)  91.1 us
    reduce_scatter x1, waiting for transfers between devices, attend(): lax.psum_scatter(key_terms, 'ctx', scatter_dimension=1, tiled=True)  54.5 us
    all_gather x1, waiting for transfers between devices, attend(): lax.all_gather(keys_in, 'ctx', axis=1, tiled=True)  45.6 us
    all_gather x1, waiting for transfers between devices, attend(): lax.all_gather(values_in, 'ctx', axis=1, tiled=True)  33.8 us
    unnamed x42, local copies, waits for them, and re-layouts  21.4 us
    ppermute x4, waiting for transfers between devices, from_partner(): return lax.ppermute(value, axis, pairs)  17.9 us
  transfers between devices with their start and end apart: 8, of which 8 were waited for; matrix products, arithmetic and copies ran while one was open for 18% of the time, Pallas kernels for 0%

commit v1 on v0

v1 whole, which is shorter than its diff:
```python
import functools
import math

import jax
import jax.numpy as jnp
from jax import lax
from jax.experimental import pallas as pl
from jax.experimental.pallas import tpu as pltpu
from jax.sharding import PartitionSpec as P

MESH = pl.DeviceIdType.MESH
HEAD = 128
RATIO = 4
CTX = 8
ROWS = 64
LENGTH = 512
BLOCK = 128
CHUNKS = 2
HEADS_PER_CHUNK = RATIO // CHUNKS
WIDTH = HEADS_PER_CHUNK * HEAD
PEERS = 2 * CTX
SCALE = HEAD ** (-0.5)
EXP2_SCALE = SCALE / math.log(2.0)
COLUMN_BLOCKS = ((0,), (0, 1), (0, 1, 2), (0, 2, 3))
BIAS_START = (0, 128, 384, 768)
BIAS_ROWS = 1152
NT_DIMS = (((1,), (1,)), ((), ()))
TN_DIMS = (((0,), (0,)), ((), ()))
NN_DIMS = (((1,), (0,)), ((), ()))


def mm(a, b, dims):
    return lax.dot_general(a, b, dims, preferred_element_type=jnp.float32)


def take_columns(ref, slot, b):
    blocks = COLUMN_BLOCKS[b]
    if blocks == tuple(range(len(blocks))):
        return ref[slot, 0 : BLOCK * len(blocks), :]
    return jnp.concatenate(
        [ref[slot, BLOCK * cb : BLOCK * (cb + 1), :] for cb in blocks], axis=0
    )


def kernel(
    q_in, k_in, v_in, g_in, lengths, tiles, flags,
    attn_out, gq_out, gk_out, gv_out,
    kbuf, vbuf, abuf, gqbuf, dk, dv, gkbuf, gvbuf, bias,
    recv_q, recv_g, recv_kv, send_q, send_g, send_kv,
    recv_out, send_a, send_gq, send_gkv,
    *chunk_bufs,
):
    qbuf, gbuf = chunk_bufs[:CHUNKS], chunk_bufs[CHUNKS:]
    dp = lax.axis_index("dp")
    c = lax.axis_index("ctx")
    half = lax.axis_size("dp") // 2
    low = dp // half
    zc = dp % half

    def peer(k):
        s = (low + k // CTX) % 2
        h = (c + k % CTX) % CTX
        return s, h, {"dp": s * half + zc, "ctx": h}

    barrier = pltpu.get_barrier_semaphore()

    @pl.loop(1, PEERS)
    def _(k):
        _, _, device = peer(k)
        pl.semaphore_signal(barrier, inc=1, device_id=device, device_id_type=MESH)

    pl.semaphore_wait(barrier, PEERS - 1)

    my_rows = pl.ds(pl.multiple_of(c * ROWS, ROWS), ROWS)

    def in_copies(j, s, h):
        wide = pl.ds(pl.multiple_of(h * (RATIO * HEAD) + j * WIDTH, WIDTH), WIDTH)
        out = [
            (q_in.at[s, :, wide], qbuf[j].at[low, my_rows, :], send_q.at[j], recv_q.at[j]),
            (g_in.at[s, :, wide], gbuf[j].at[low, my_rows, :], send_g.at[j], recv_g.at[j]),
        ]
        if j == 0:
            thin = pl.ds(pl.multiple_of(h * HEAD, HEAD), HEAD)
            out = [
                (k_in.at[s, :, thin], kbuf.at[low, my_rows, :], send_kv.at[0], recv_kv.at[0]),
                (v_in.at[s, :, thin], vbuf.at[low, my_rows, :], send_kv.at[1], recv_kv.at[1]),
            ] + out
        return out

    def start_remote(copies, device):
        for src, dst, send, recv in copies:
            pltpu.make_async_remote_copy(
                src_ref=src, dst_ref=dst, send_sem=send, recv_sem=recv,
                device_id=device, device_id_type=MESH,
            ).start()

    def start_local(copies):
        for src, dst, _, recv in copies:
            pltpu.make_async_copy(src, dst, recv).start()

    for j in range(CHUNKS):

        @pl.loop(1, PEERS)
        def _(k, j=j):
            s, h, device = peer(k)
            start_remote(in_copies(j, s, h), device)

        start_local(in_copies(j, low, c))

    flag = jnp.where(flags[dp] == 1, 1, 0) * low
    lane = lax.broadcasted_iota(jnp.int32, (BLOCK, BLOCK), 1)
    sub = lax.broadcasted_iota(jnp.int32, (BLOCK, BLOCK), 0)

    def source(slot):
        return slot + flag - 2 * slot * flag

    @pl.loop(0, 2)
    def _(slot):
        seq = 2 * (source(slot) * half + zc) + low
        ends = []
        total = lengths[seq, 0]
        for d in range(1, 8):
            ends.append(total)
            total = total + lengths[seq, d]
        for b in range(4):
            row = lane + BLOCK * b
            row_doc = sum((row >= e).astype(jnp.int32) for e in ends)
            for n, cb in enumerate(COLUMN_BLOCKS[b]):
                col = sub + BLOCK * cb
                col_doc = sum((col >= e).astype(jnp.int32) for e in ends)
                first = jnp.where(lane < 64, tiles[seq, 2 * b, 2 * cb], tiles[seq, 2 * b + 1, 2 * cb])
                second = jnp.where(
                    lane < 64, tiles[seq, 2 * b, 2 * cb + 1], tiles[seq, 2 * b + 1, 2 * cb + 1]
                )
                tile = jnp.where(sub < 64, first, second)
                allowed = (col <= row) & ((col_doc == row_doc) | (col_doc == 0)) & (tile == 1)
                at = BIAS_START[b] + BLOCK * n
                bias[slot, at : at + BLOCK, :] = jnp.where(allowed, 0.0, -1e30)

    dk[...] = jnp.zeros_like(dk)
    dv[...] = jnp.zeros_like(dv)

    pltpu.make_async_copy(kbuf, kbuf, recv_kv.at[0]).wait()
    pltpu.make_async_copy(vbuf, vbuf, recv_kv.at[1]).wait()

    def add_columns(ref, slot, b, value):
        for n, cb in enumerate(COLUMN_BLOCKS[b]):
            ref[slot, BLOCK * cb : BLOCK * (cb + 1), :] += value[BLOCK * n : BLOCK * (n + 1)]

    def out_copies(j, s, h):
        rows = pl.ds(pl.multiple_of(h * ROWS, ROWS), ROWS)
        wide = pl.ds(pl.multiple_of(c * (RATIO * HEAD) + j * WIDTH, WIDTH), WIDTH)
        return [
            (abuf.at[j, s, rows, :], attn_out.at[low, :, wide], send_a.at[j], recv_out.at[0]),
            (gqbuf.at[j, s, rows, :], gq_out.at[low, :, wide], send_gq.at[j], recv_out.at[1]),
        ]

    def kv_copies(s, h):
        rows = pl.ds(pl.multiple_of(h * ROWS, ROWS), ROWS)
        thin = pl.ds(pl.multiple_of(c * HEAD, HEAD), HEAD)
        return [
            (gkbuf.at[s, rows, :], gk_out.at[low, :, thin], send_gkv.at[0], recv_out.at[2]),
            (gvbuf.at[s, rows, :], gv_out.at[low, :, thin], send_gkv.at[1], recv_out.at[3]),
        ]

    for j in range(CHUNKS):
        pltpu.make_async_copy(qbuf[j], qbuf[j], recv_q.at[j]).wait()
        pltpu.make_async_copy(gbuf[j], gbuf[j], recv_g.at[j]).wait()

        @pl.loop(0, 2)
        def _(slot, j=j):
            u = source(slot)
            for b in range(4):
                rows = slice(BLOCK * b, BLOCK * (b + 1))
                n_cols = BLOCK * len(COLUMN_BLOCKS[b])
                keys = take_columns(kbuf, u, b)
                values = take_columns(vbuf, u, b)
                heads = [slice(HEAD * h, HEAD * (h + 1)) for h in range(HEADS_PER_CHUNK)]
                queries = jnp.concatenate([qbuf[j][u, rows, h] for h in heads], axis=0)
                grads = jnp.concatenate([gbuf[j][u, rows, h] for h in heads], axis=0)
                mask = bias[slot, BIAS_START[b] : BIAS_START[b] + n_cols, :]
                mask = jnp.concatenate([mask] * HEADS_PER_CHUNK, axis=1)
                scores = mm(keys, queries, NT_DIMS) + mask
                peak = jnp.max(scores, axis=0, keepdims=True)
                expd = jnp.exp2((scores - peak) * EXP2_SCALE)
                probs = expd * (1.0 / jnp.sum(expd, axis=0, keepdims=True))
                probs_b = probs.astype(jnp.bfloat16)
                dprobs = mm(values, grads, NT_DIMS)
                delta = jnp.sum(probs * dprobs, axis=0, keepdims=True)
                dscores = (probs * (dprobs - delta)).astype(jnp.bfloat16)
                attn = mm(probs_b, values, TN_DIMS).astype(jnp.bfloat16)
                gq = (mm(dscores, keys, TN_DIMS) * SCALE).astype(jnp.bfloat16)
                for n, h in enumerate(heads):
                    abuf[j, slot, rows, h] = attn[BLOCK * n : BLOCK * (n + 1)]
                    gqbuf[j, slot, rows, h] = gq[BLOCK * n : BLOCK * (n + 1)]
                add_columns(dv, slot, b, mm(probs_b, grads, NN_DIMS))
                add_columns(dk, slot, b, mm(dscores, queries, NN_DIMS))

        if j == CHUNKS - 1:
            gkbuf[...] = (dk[...] * SCALE).astype(jnp.bfloat16)
            gvbuf[...] = dv[...].astype(jnp.bfloat16)

        @pl.loop(1, PEERS)
        def _(k, j=j):
            s, h, device = peer(k)
            start_remote(out_copies(j, s, h), device)
            if j == CHUNKS - 1:
                start_remote(kv_copies(s, h), device)

        start_local(out_copies(j, low, c))
        if j == CHUNKS - 1:
            start_local(kv_copies(low, c))

    sent = pl.ds(0, LENGTH - ROWS // 2)
    for j in range(CHUNKS):
        for buf, sem in (
            (qbuf[j], send_q), (gbuf[j], send_g), (abuf.at[j], send_a), (gqbuf.at[j], send_gq)
        ):
            part = buf.at[:, sent, :]
            pltpu.make_async_copy(part, part, sem.at[j]).wait()
    for buf, sem in (
        (kbuf, send_kv.at[0]), (vbuf, send_kv.at[1]), (gkbuf, send_gkv.at[0]), (gvbuf, send_gkv.at[1])
    ):
        part = buf.at[:, sent, :]
        pltpu.make_async_copy(part, part, sem).wait()
    for n, ref in enumerate((attn_out, gq_out, gk_out, gv_out)):
        pltpu.make_async_copy(ref, ref, recv_out.at[n]).wait()


def shards(query_proj, key_proj, value_proj, grad_attn, doc_lengths, mask_tiles, pair_flags):
    bf16, f32 = jnp.bfloat16, jnp.float32
    dma = pltpu.SemaphoreType.DMA
    anywhere = pl.BlockSpec(memory_space=pl.ANY)
    scalars = pl.BlockSpec(memory_space=pltpu.SMEM)
    wide = pltpu.VMEM((CHUNKS, 2, LENGTH, WIDTH), bf16)
    chunk = pltpu.VMEM((2, LENGTH, WIDTH), bf16)
    thin = pltpu.VMEM((2, LENGTH, HEAD), bf16)
    total = pltpu.VMEM((2, LENGTH, HEAD), f32)
    return pl.pallas_call(
        kernel,
        out_shape=tuple(
            jax.ShapeDtypeStruct(a.shape, bf16)
            for a in (query_proj, query_proj, key_proj, value_proj)
        ),
        in_specs=[anywhere] * 4 + [scalars] * 3,
        out_specs=(anywhere,) * 4,
        scratch_shapes=[
            thin, thin, wide, wide, total, total, thin, thin,
            pltpu.VMEM((2, BIAS_ROWS, BLOCK), f32),
            dma((CHUNKS,)), dma((CHUNKS,)), dma((2,)),
            dma((CHUNKS,)), dma((CHUNKS,)), dma((2,)),
            dma((4,)), dma((CHUNKS,)), dma((CHUNKS,)), dma((2,)),
            *[chunk] * (2 * CHUNKS),
        ],
        compiler_params=pltpu.CompilerParams(
            collective_id=0, has_side_effects=True, vmem_limit_bytes=48 * 2**20
        ),
    )(query_proj, key_proj, value_proj, grad_attn, doc_lengths, mask_tiles, pair_flags)


def solution(mesh):
    split = P("dp", "ctx", None)
    return jax.shard_map(
        shards,
        mesh=mesh,
        in_specs=(split,) * 4 + (P(),) * 3,
        out_specs=(split,) * 4,
        check_vma=False,
    )
```

time: 380 us -> 82.1 us (0.22)
  waiting for transfers between devices: 243 us -> 0 us
  Pallas kernels: 0 us -> 73 us
  local copies, waits for them, and re-layouts: 71.7 us -> 8.22 us
  matrix products: 22.5 us -> 0 us
  other arithmetic: 22.4 us -> 0 us
  between operations: 14.8 us -> 0.68 us
  starting transfers between devices: 4.39 us -> 0 us
    reduce_scatter x2 -> x0, waiting for transfers between devices: 146 us -> none  [the longest x1 91.1 us: attend(): lax.psum_scatter(value_terms, 'ctx', scatter_dimension=1, tiled=True)]
    all_gather x2 -> x0, waiting for transfers between devices: 79.4 us -> none  [the longest x1 45.6 us: attend(): lax.all_gather(keys_in, 'ctx', axis=1, tiled=True)]
    pallas_call x0 -> x1, Pallas kernels: none -> 73 us  [shards(): pl.pallas_call(kernel, out_shape=tuple((jax.ShapeDtypeStruct(a.shape, bf1...]
    another operation x14 -> x0, local copies, waits for them, and re-layouts: 23.6 us -> none  [the longest x2 5.82 us: attend(): value_terms = jnp.stack([pieces[0][3], pieces[1][3]])]
    dot_general x14 -> x0, matrix products: 22.5 us -> none  [the longest x2 6.97 us: sequence_core(): jnp.einsum('grij,igrd->jgd', probs_b, head_gradients, preferred_element_t...]
    slice x6 -> x0, local copies, waits for them, and re-layouts: 18.1 us -> none  [the longest x1 6.56 us: attend(): values_all[seq_slot]]
    ppermute x4 -> x0, waiting for transfers between devices: 17.9 us -> none  [from_partner(): return lax.ppermute(value, axis, pairs)]
    unnamed x42 -> x18, local copies, waits for them, and re-layouts: 21.4 us -> 8.22 us
  transfers between devices with their start and end apart: 8 -> 0, of which waited for: 8 -> 0; matrix products, arithmetic and copies ran while one was open for 18% -> 0% of each run, Pallas kernels for 0% -> 0%
where the time goes in v1:
time: 82.1 us; the launch traced here: 81.9 us
  Pallas kernels  73 us (89%)
  local copies, waits for them, and re-layouts  8.22 us (10%)
    pallas_call x1, Pallas kernels, shards(): pl.pallas_call(kernel, out_shape=tuple((jax.ShapeDtypeStruct(a.shape, bf1...  73 us
    unnamed x18, local copies, waits for them, and re-layouts  8.22 us

profile of v1, /device:TPU:64, one launch (start us, length us, event | category | flops | bytes accessed | tf_op | source)
XLA Modules:
  0.0 81.9 jit_solution(13304556054011367674)
XLA Ops:
  0.6 0.0 copy-start.5
  0.6 0.0 copy-start.2
  0.7 0.8 copy.11.lengths
  1.5 0.0 copy-done.5
  1.5 0.0 copy-start.4
  1.5 0.1 copy.12.tiles
  1.6 0.0 copy-done.2
  1.6 0.5 copy-done.4
  2.1 0.0 copy-start
  2.1 1.2 %copy-done = bf16[2,64,4096]{2,1,0:T(8,128)(2,1)S(1)} copy-done((bf16[2,64,4096]{2,1,0:T(8,128)(2,1)S(1)}, bf16[2,64,4096]{2,1,0:T(8,128)(2,1)}, u32[]{:S(2)}) %copy-start) | copy-done | bytes 1048600
  3.4 0.0 copy-start.1
  3.4 1.2 %copy-done.1 = bf16[2,64,4096]{2,1,0:T(8,128)(2,1)S(1)} copy-done((bf16[2,64,4096]{2,1,0:T(8,128)(2,1)S(1)}, bf16[2,64,4096]{2,1,0:T(8,128)(2,1)}, u32[]{:S(2)}) %copy-start.1) | copy-done | bytes 1048600
  4.6 0.0 copy-start.3
  4.6 0.9 %copy-done.3 = bf16[2,64,1024]{2,1,0:T(8,128)(2,1)S(1)} copy-done((bf16[2,64,1024]{2,1,0:T(8,128)(2,1)S(1)}, bf16[2,64,1024]{2,1,0:T(8,128)(2,1)}, u32[]{:S(2)}) %copy-start.3) | copy-done | bytes 262168
  5.5 73.0 %shard_map.102 = (bf16[2,64,4096]{2,1,0:T(8,128)(2,1)S(1)}, bf16[2,64,4096]{2,1,0:T(8,128)(2,1)S(1)}, bf16[2,64,1024]{2,1,0:T(8,128)(2,1)S(1)}, bf16[2,64,1024]{2,1,0:T(8,128)(2,1)S(1)}) custom-call(bf16[2,64,4096]{2,1,0:T(8,128)(2,1)S(1)} %copy-done, bf16[2,64,1024]{2,1,0:T(8,128)(2,1)S(1)} %copy-done.2, bf16[2,64,1024]{2,1,0:T(8,128)(2,1)S(1)} %copy-done.3, ...), custom_call_target="tpu_custom_call" | custom-call | tf_op jit(solution)/shard_map/pallas_call | solution.py:239
  78.5 1.0 %copy.17 = bf16[2,64,4096]{2,1,0:T(8,128)(2,1)} copy(bf16[2,64,4096]{2,1,0:T(8,128)(2,1)S(1)} %get-tuple-element.8) | data formatting | bytes 2097152
  79.5 1.0 %copy.18 = bf16[2,64,4096]{2,1,0:T(8,128)(2,1)} copy(bf16[2,64,4096]{2,1,0:T(8,128)(2,1)S(1)} %get-tuple-element.9) | data formatting | bytes 2097152
  80.5 0.7 copy.19
  81.2 0.7 copy.20
Async XLA Ops:
  0.6 0.8 %copy-start.5 = (s32[64,8,8]{0,2,1:T(8,128)S(1)}, s32[64,8,8]{0,2,1:T(8,128)}, u32[]{:S(2)}) copy-start(s32[64,8,8]{0,2,1:T(8,128)} %param.12) | copy-start | bytes 49156
  0.6 1.0 %copy-start.2 = (bf16[2,64,1024]{2,1,0:T(8,128)(2,1)S(1)}, bf16[2,64,1024]{2,1,0:T(8,128)(2,1)}, u32[]{:S(2)}) copy-start(bf16[2,64,1024]{2,1,0:T(8,128)(2,1)} %k_in.1) | copy-start | bytes 786436
  1.5 0.7 copy-start.4
  2.1 1.2 %copy-start = (bf16[2,64,4096]{2,1,0:T(8,128)(2,1)S(1)}, bf16[2,64,4096]{2,1,0:T(8,128)(2,1)}, u32[]{:S(2)}) copy-start(bf16[2,64,4096]{2,1,0:T(8,128)(2,1)} %q_in.1) | copy-start | bytes 3145732
  3.4 1.2 %copy-start.1 = (bf16[2,64,4096]{2,1,0:T(8,128)(2,1)S(1)}, bf16[2,64,4096]{2,1,0:T(8,128)(2,1)}, u32[]{:S(2)}) copy-start(bf16[2,64,4096]{2,1,0:T(8,128)(2,1)} %g_in.1) | copy-start | bytes 3145732
  4.6 0.9 %copy-start.3 = (bf16[2,64,1024]{2,1,0:T(8,128)(2,1)S(1)}, bf16[2,64,1024]{2,1,0:T(8,128)(2,1)}, u32[]{:S(2)}) copy-start(bf16[2,64,1024]{2,1,0:T(8,128)(2,1)} %v_in.1) | copy-start | bytes 786436

commit v2 on v1

--- a/solution.py
+++ b/solution.py
@@ -19,6 +19,10 @@
 HEADS_PER_CHUNK = RATIO // CHUNKS
 WIDTH = HEADS_PER_CHUNK * HEAD
 PEERS = 2 * CTX
+ORDER = (
+    (1, 1), (3, 3), (2, 2), (0, 1), (1, 0), (3, 2), (2, 3), (0, 2),
+    (3, 1), (1, 2), (2, 0), (0, 3), (1, 3), (3, 0), (2, 1),
+)
 SCALE = HEAD ** (-0.5)
 EXP2_SCALE = SCALE / math.log(2.0)
 COLUMN_BLOCKS = ((0,), (0, 1), (0, 1, 2), (0, 2, 3))
@@ -57,16 +61,16 @@
     low = dp // half
     zc = dp % half
 
-    def peer(k):
-        s = (low + k // CTX) % 2
-        h = (c + k % CTX) % CTX
+    def peer(step):
+        dx, dy = step
+        s = (low + dy % 2) % 2
+        h = (c // 4 + dy // 2) % 2 * 4 + (c % 4 + dx) % 4
         return s, h, {"dp": s * half + zc, "ctx": h}
 
     barrier = pltpu.get_barrier_semaphore()
 
-    @pl.loop(1, PEERS)
-    def _(k):
-        _, _, device = peer(k)
+    for step in ORDER:
+        _, _, device = peer(step)
         pl.semaphore_signal(barrier, inc=1, device_id=device, device_id_type=MESH)
 
     pl.semaphore_wait(barrier, PEERS - 1)
@@ -99,10 +103,8 @@
             pltpu.make_async_copy(src, dst, recv).start()
 
     for j in range(CHUNKS):
-
-        @pl.loop(1, PEERS)
-        def _(k, j=j):
-            s, h, device = peer(k)
+        for step in ORDER:
+            s, h, device = peer(step)
             start_remote(in_copies(j, s, h), device)
 
         start_local(in_copies(j, low, c))
@@ -118,19 +120,19 @@
     def _(slot):
         seq = 2 * (source(slot) * half + zc) + low
         ends = []
-        total = lengths[seq, 0]
+        total = lengths[0, seq]
         for d in range(1, 8):
             ends.append(total)
-            total = total + lengths[seq, d]
+            total = total + lengths[d, seq]
         for b in range(4):
             row = lane + BLOCK * b
             row_doc = sum((row >= e).astype(jnp.int32) for e in ends)
             for n, cb in enumerate(COLUMN_BLOCKS[b]):
                 col = sub + BLOCK * cb
                 col_doc = sum((col >= e).astype(jnp.int32) for e in ends)
-                first = jnp.where(lane < 64, tiles[seq, 2 * b, 2 * cb], tiles[seq, 2 * b + 1, 2 * cb])
+                first = jnp.where(lane < 64, tiles[2 * b, 2 * cb, seq], tiles[2 * b + 1, 2 * cb, seq])
                 second = jnp.where(
-                    lane < 64, tiles[seq, 2 * b, 2 * cb + 1], tiles[seq, 2 * b + 1, 2 * cb + 1]
+                    lane < 64, tiles[2 * b, 2 * cb + 1, seq], tiles[2 * b + 1, 2 * cb + 1, seq]
                 )
                 tile = jnp.where(sub < 64, first, second)
                 allowed = (col <= row) & ((col_doc == row_doc) | (col_doc == 0)) & (tile == 1)
@@ -200,9 +202,8 @@
             gkbuf[...] = (dk[...] * SCALE).astype(jnp.bfloat16)
             gvbuf[...] = dv[...].astype(jnp.bfloat16)
 
-        @pl.loop(1, PEERS)
-        def _(k, j=j):
-            s, h, device = peer(k)
+        for step in ORDER:
+            s, h, device = peer(step)
             start_remote(out_copies(j, s, h), device)
             if j == CHUNKS - 1:
                 start_remote(kv_copies(s, h), device)
@@ -236,7 +237,7 @@
     chunk = pltpu.VMEM((2, LENGTH, WIDTH), bf16)
     thin = pltpu.VMEM((2, LENGTH, HEAD), bf16)
     total = pltpu.VMEM((2, LENGTH, HEAD), f32)
-    return pl.pallas_call(
+    return finish(pl.pallas_call(
         kernel,
         out_shape=tuple(
             jax.ShapeDtypeStruct(a.shape, bf16)
@@ -255,7 +256,32 @@
         compiler_params=pltpu.CompilerParams(
             collective_id=0, has_side_effects=True, vmem_limit_bytes=48 * 2**20
         ),
-    )(query_proj, key_proj, value_proj, grad_attn, doc_lengths, mask_tiles, pair_flags)
+    )(*[
+        pltpu.with_memory_space_constraint(x, pltpu.HBM)
+        for x in (
+            query_proj, key_proj, value_proj, grad_attn,
+            doc_lengths.T, jnp.transpose(mask_tiles, (1, 2, 0)), pair_flags,
+        )
+    ]))
+
+
+def finish_kernel(*refs):
+    ins, outs, sem = refs[:4], refs[4:8], refs[8]
+    for n in range(4):
+        pltpu.make_async_copy(ins[n], outs[n], sem.at[n]).start()
+    for n in range(4):
+        pltpu.make_async_copy(ins[n], outs[n], sem.at[n]).wait()
+
+
+def finish(arrays):
+    anywhere = pl.BlockSpec(memory_space=pl.ANY)
+    return pl.pallas_call(
+        finish_kernel,
+        out_shape=tuple(jax.ShapeDtypeStruct(a.shape, a.dtype) for a in arrays),
+        in_specs=[anywhere] * 4,
+        out_specs=(anywhere,) * 4,
+        scratch_shapes=[pltpu.SemaphoreType.DMA((4,))],
+    )(*[pltpu.with_memory_space_constraint(x, pltpu.VMEM) for x in arrays])
 
 
 def solution(mesh):

time: 82.1 us -> 71.8 us (0.87)
  local copies, waits for them, and re-layouts: 8.22 us -> 0 us
  Pallas kernels: 73 us -> 70.6 us
    unnamed x18 -> x0, local copies, waits for them, and re-layouts: 8.22 us -> none
    pallas_call x1, Pallas kernels: 73 us -> 69.1 us  [shards(): pl.pallas_call(kernel, out_shape=tuple((jax.ShapeDtypeStruct(a.shape, bf1...]
    pallas_call x0 -> x1, Pallas kernels: none -> 1.52 us  [finish(): pl.pallas_call(finish_kernel, out_shape=tuple((jax.ShapeDtypeStruct(a.sha...]
where the time goes in v2:
time: 71.8 us; the launch traced here: 71.2 us
  Pallas kernels  70.6 us (98%)
    pallas_call x1, Pallas kernels, shards(): pl.pallas_call(kernel, out_shape=tuple((jax.ShapeDtypeStruct(a.shape, bf1...  69.1 us
    pallas_call x1, Pallas kernels, finish(): pl.pallas_call(finish_kernel, out_shape=tuple((jax.ShapeDtypeStruct(a.sha...  1.52 us

profile of v2, /device:TPU:64, one launch (start us, length us, event | category | flops | bytes accessed | tf_op | source)
XLA Modules:
  0.0 71.2 jit_solution(15590901350163211758)
XLA Ops:
  0.6 69.1 %shard_map.102 = (bf16[2,64,4096]{2,1,0:T(8,128)(2,1)S(1)}, bf16[2,64,4096]{2,1,0:T(8,128)(2,1)S(1)}, bf16[2,64,1024]{2,1,0:T(8,128)(2,1)S(1)}, bf16[2,64,1024]{2,1,0:T(8,128)(2,1)S(1)}) custom-call(bf16[2,64,4096]{2,1,0:T(8,128)(2,1)} %q_in.1, bf16[2,64,1024]{2,1,0:T(8,128)(2,1)} %k_in.1, bf16[2,64,1024]{2,1,0:T(8,128)(2,1)} %v_in.1, ...), custom_call_target="tpu_custom_call" | custom-call | tf_op jit(solution)/shard_map/pallas_call | solution.py:240
  69.7 1.5 %shard_map.103 = (bf16[2,64,4096]{2,1,0:T(8,128)(2,1)}, bf16[2,64,4096]{2,1,0:T(8,128)(2,1)}, bf16[2,64,1024]{2,1,0:T(8,128)(2,1)}, bf16[2,64,1024]{2,1,0:T(8,128)(2,1)}) custom-call(bf16[2,64,4096]{2,1,0:T(8,128)(2,1)S(1)} %get-tuple-element.8.refs_0_, bf16[2,64,4096]{2,1,0:T(8,128)(2,1)S(1)} %get-tuple-element.9.refs_1_, ...), custom_call_target="tpu_custom_call" | custom-call | tf_op jit(solution)/shard_map/pallas_call | solution.py:278

commit v3 on v2

--- a/solution.py
+++ b/solution.py
@@ -15,7 +15,7 @@
 ROWS = 64
 LENGTH = 512
 BLOCK = 128
-CHUNKS = 2
+CHUNKS = 4
 HEADS_PER_CHUNK = RATIO // CHUNKS
 WIDTH = HEADS_PER_CHUNK * HEAD
 PEERS = 2 * CTX

time: 71.8 us -> 67.9 us (0.946)
  Pallas kernels: 70.6 us -> 67.1 us
    pallas_call x1, Pallas kernels: 69.1 us -> 65.6 us  [shards(): pl.pallas_call(kernel, out_shape=tuple((jax.ShapeDtypeStruct(a.shape, bf1...]
where the time goes in v3:
time: 67.9 us; the launch traced here: 67.7 us
  Pallas kernels  67.1 us (99%)
    pallas_call x1, Pallas kernels, shards(): pl.pallas_call(kernel, out_shape=tuple((jax.ShapeDtypeStruct(a.shape, bf1...  65.6 us
    pallas_call x1, Pallas kernels, finish(): pl.pallas_call(finish_kernel, out_shape=tuple((jax.ShapeDtypeStruct(a.sha...  1.52 us

profile of v3, /device:TPU:64, one launch (start us, length us, event | category | flops | bytes accessed | tf_op | source)
XLA Modules:
  0.0 67.7 jit_solution(15028662151115519253)
XLA Ops:
  0.6 65.6 %shard_map.102 = (bf16[2,64,4096]{2,1,0:T(8,128)(2,1)S(1)}, bf16[2,64,4096]{2,1,0:T(8,128)(2,1)S(1)}, bf16[2,64,1024]{2,1,0:T(8,128)(2,1)S(1)}, bf16[2,64,1024]{2,1,0:T(8,128)(2,1)S(1)}) custom-call(bf16[2,64,4096]{2,1,0:T(8,128)(2,1)} %q_in.1, bf16[2,64,1024]{2,1,0:T(8,128)(2,1)} %k_in.1, bf16[2,64,1024]{2,1,0:T(8,128)(2,1)} %v_in.1, ...), custom_call_target="tpu_custom_call" | custom-call | tf_op jit(solution)/shard_map/pallas_call | solution.py:240
  66.2 1.5 %shard_map.103 = (bf16[2,64,4096]{2,1,0:T(8,128)(2,1)}, bf16[2,64,4096]{2,1,0:T(8,128)(2,1)}, bf16[2,64,1024]{2,1,0:T(8,128)(2,1)}, bf16[2,64,1024]{2,1,0:T(8,128)(2,1)}) custom-call(bf16[2,64,4096]{2,1,0:T(8,128)(2,1)S(1)} %get-tuple-element.8.refs_0_, bf16[2,64,4096]{2,1,0:T(8,128)(2,1)S(1)} %get-tuple-element.9.refs_1_, ...), custom_call_target="tpu_custom_call" | custom-call | tf_op jit(solution)/shard_map/pallas_call | solution.py:278

commit v4 on v3

--- a/solution.py
+++ b/solution.py
@@ -47,11 +47,12 @@
 
 
 def kernel(
-    q_in, k_in, v_in, g_in, lengths, tiles, flags,
+    q_in, k_in, v_in, g_in, lengths_in, tiles_in, flags_in,
     attn_out, gq_out, gk_out, gv_out,
     kbuf, vbuf, abuf, gqbuf, dk, dv, gkbuf, gvbuf, bias,
     recv_q, recv_g, recv_kv, send_q, send_g, send_kv,
     recv_out, send_a, send_gq, send_gkv,
+    lengths, tiles, flags, scalar_sem,
     *chunk_bufs,
 ):
     qbuf, gbuf = chunk_bufs[:CHUNKS], chunk_bufs[CHUNKS:]
@@ -66,6 +67,13 @@
         s = (low + dy % 2) % 2
         h = (c // 4 + dy // 2) % 2 * 4 + (c % 4 + dx) % 4
         return s, h, {"dp": s * half + zc, "ctx": h}
+
+    scalar_copies = [
+        pltpu.make_async_copy(src, dst, scalar_sem.at[n])
+        for n, (src, dst) in enumerate(((lengths_in, lengths), (tiles_in, tiles), (flags_in, flags)))
+    ]
+    for copy in scalar_copies:
+        copy.start()
 
     barrier = pltpu.get_barrier_semaphore()
 
@@ -109,6 +117,8 @@
 
         start_local(in_copies(j, low, c))
 
+    for copy in scalar_copies:
+        copy.wait()
     flag = jnp.where(flags[dp] == 1, 1, 0) * low
     lane = lax.broadcasted_iota(jnp.int32, (BLOCK, BLOCK), 1)
     sub = lax.broadcasted_iota(jnp.int32, (BLOCK, BLOCK), 0)
@@ -232,7 +242,7 @@
     bf16, f32 = jnp.bfloat16, jnp.float32
     dma = pltpu.SemaphoreType.DMA
     anywhere = pl.BlockSpec(memory_space=pl.ANY)
-    scalars = pl.BlockSpec(memory_space=pltpu.SMEM)
+    scalars = (doc_lengths.T, jnp.transpose(mask_tiles, (1, 2, 0)), pair_flags)
     wide = pltpu.VMEM((CHUNKS, 2, LENGTH, WIDTH), bf16)
     chunk = pltpu.VMEM((2, LENGTH, WIDTH), bf16)
     thin = pltpu.VMEM((2, LENGTH, HEAD), bf16)
@@ -243,7 +253,7 @@
             jax.ShapeDtypeStruct(a.shape, bf16)
             for a in (query_proj, query_proj, key_proj, value_proj)
         ),
-        in_specs=[anywhere] * 4 + [scalars] * 3,
+        in_specs=[anywhere] * 7,
         out_specs=(anywhere,) * 4,
         scratch_shapes=[
             thin, thin, wide, wide, total, total, thin, thin,
@@ -251,6 +261,7 @@
             dma((CHUNKS,)), dma((CHUNKS,)), dma((2,)),
             dma((CHUNKS,)), dma((CHUNKS,)), dma((2,)),
             dma((4,)), dma((CHUNKS,)), dma((CHUNKS,)), dma((2,)),
+            *[pltpu.SMEM(a.shape, a.dtype) for a in scalars], dma((3,)),
             *[chunk] * (2 * CHUNKS),
         ],
         compiler_params=pltpu.CompilerParams(
@@ -258,10 +269,7 @@
         ),
     )(*[
         pltpu.with_memory_space_constraint(x, pltpu.HBM)
-        for x in (
-            query_proj, key_proj, value_proj, grad_attn,
-            doc_lengths.T, jnp.transpose(mask_tiles, (1, 2, 0)), pair_flags,
-        )
+        for x in (query_proj, key_proj, value_proj, grad_attn, *scalars)
     ]))
 
 

time: 67.9 us -> 66.6 us (0.981)
  Pallas kernels: 67.1 us -> 65.8 us
    pallas_call x1, Pallas kernels: 65.6 us -> 64.3 us  [shards(): pl.pallas_call(kernel, out_shape=tuple((jax.ShapeDtypeStruct(a.shape, bf1...]
where the time goes in v4:
time: 66.6 us; the launch traced here: 66.5 us
  Pallas kernels  65.8 us (99%)
    pallas_call x1, Pallas kernels, shards(): pl.pallas_call(kernel, out_shape=tuple((jax.ShapeDtypeStruct(a.shape, bf1...  64.3 us
    pallas_call x1, Pallas kernels, finish(): pl.pallas_call(finish_kernel, out_shape=tuple((jax.ShapeDtypeStruct(a.sha...  1.52 us

profile of v4, /device:TPU:64, one launch (start us, length us, event | category | flops | bytes accessed | tf_op | source)
XLA Modules:
  0.0 66.5 jit_solution(15106575947104123306)
XLA Ops:
  0.6 64.3 %shard_map.102 = (bf16[2,64,4096]{2,1,0:T(8,128)(2,1)S(1)}, bf16[2,64,4096]{2,1,0:T(8,128)(2,1)S(1)}, bf16[2,64,1024]{2,1,0:T(8,128)(2,1)S(1)}, bf16[2,64,1024]{2,1,0:T(8,128)(2,1)S(1)}) custom-call(bf16[2,64,4096]{2,1,0:T(8,128)(2,1)} %q_in.1, bf16[2,64,1024]{2,1,0:T(8,128)(2,1)} %k_in.1, bf16[2,64,1024]{2,1,0:T(8,128)(2,1)} %v_in.1, ...), custom_call_target="tpu_custom_call" | custom-call | tf_op jit(solution)/shard_map/pallas_call | solution.py:250
  65.0 1.5 %shard_map.103 = (bf16[2,64,4096]{2,1,0:T(8,128)(2,1)}, bf16[2,64,4096]{2,1,0:T(8,128)(2,1)}, bf16[2,64,1024]{2,1,0:T(8,128)(2,1)}, bf16[2,64,1024]{2,1,0:T(8,128)(2,1)}) custom-call(bf16[2,64,4096]{2,1,0:T(8,128)(2,1)S(1)} %get-tuple-element.8.refs_0_, bf16[2,64,4096]{2,1,0:T(8,128)(2,1)S(1)} %get-tuple-element.9.refs_1_, ...), custom_call_target="tpu_custom_call" | custom-call | tf_op jit(solution)/shard_map/pallas_call | solution.py:286

commit v5 on v4

v5 whole, which is shorter than its diff:
```python
import functools
import math

import jax
import jax.numpy as jnp
from jax import lax
from jax.experimental import pallas as pl
from jax.experimental.pallas import tpu as pltpu
from jax.sharding import PartitionSpec as P

MESH = pl.DeviceIdType.MESH
HEAD = 128
RATIO = 4
ROWS = 64
LENGTH = 512
BLOCK = 128
SIDE = 4
PAIR = 2 * HEAD
QPAIR = RATIO * PAIR
E_CHUNKS = 4
E_WIDTH = QPAIR // E_CHUNKS
O_CHUNKS = 2
O_WIDTH = QPAIR // O_CHUNKS
SCALE = HEAD ** (-0.5)
EXP2_SCALE = SCALE / math.log(2.0)
COLUMN_BLOCKS = ((0,), (0, 1), (0, 1, 2), (0, 2, 3))
BIAS_START = (0, 128, 0, 384)
NT_DIMS = (((1,), (1,)), ((), ()))
TN_DIMS = (((0,), (0,)), ((), ()))
NN_DIMS = (((1,), (0,)), ((), ()))
STEPS = (1, 3, 2)


def mm(a, b, dims):
    return lax.dot_general(a, b, dims, preferred_element_type=jnp.float32)


def attend(queries, grads, keys, values, mask):
    scores = mm(keys, queries, NT_DIMS) + mask
    peak = jnp.max(scores, axis=0, keepdims=True)
    expd = jnp.exp2((scores - peak) * EXP2_SCALE)
    probs = expd * (1.0 / jnp.sum(expd, axis=0, keepdims=True))
    probs_b = probs.astype(jnp.bfloat16)
    dprobs = mm(values, grads, NT_DIMS)
    delta = jnp.sum(probs * dprobs, axis=0, keepdims=True)
    dscores = (probs * (dprobs - delta)).astype(jnp.bfloat16)
    attn = mm(probs_b, values, TN_DIMS).astype(jnp.bfloat16)
    gq = (mm(dscores, keys, TN_DIMS) * SCALE).astype(jnp.bfloat16)
    return attn, gq, mm(dscores, queries, NN_DIMS), mm(probs_b, grads, NN_DIMS)


def kernel(
    q_in, k_in, v_in, g_in, lengths_in, tiles_in, flags_in,
    attn_out, gq_out, gk_out, gv_out,
    ek, ev, ok, ov, ea, egq, oa, ogq, edk, edv, odk, odv, ebias, obias,
    esk, esv, erk, erv, egk, egv, opk, opv, rpk, rpv, ogk, ogv,
    lengths, tiles, flags, scalar_sem,
    r_eq, r_eg, r_oq, r_og, r_kv, r_all, r_fwd, r_ep, r_rs, r_out,
    s_eq, s_eg, s_oq, s_og, s_kv, s_all, s_fwd, s_ep, s_rs,
    s_ea, s_egq, s_oa, s_ogq, s_gkv,
    *bufs,
):
    eq, eg = bufs[0:E_CHUNKS], bufs[E_CHUNKS : 2 * E_CHUNKS]
    oq, og = bufs[2 * E_CHUNKS : 2 * E_CHUNKS + O_CHUNKS], bufs[2 * E_CHUNKS + O_CHUNKS :]
    dp = lax.axis_index("dp")
    c = lax.axis_index("ctx")
    half = lax.axis_size("dp") // 2
    low = dp // half
    zc = dp % half
    hi = c // SIDE
    x = c % SIDE
    y = 2 * hi + low

    def along_x(step):
        xn = (x + step) % SIDE
        return xn, {"dp": dp, "ctx": hi * SIDE + xn}

    def along_y(step):
        yn = (y + step) % SIDE
        return yn, {"dp": (yn % 2) * half + zc, "ctx": (yn // 2) * SIDE + x}

    def across(device_hi):
        return {"dp": dp, "ctx": device_hi * SIDE + x}

    scalar_copies = [
        pltpu.make_async_copy(src, dst, scalar_sem.at[n])
        for n, (src, dst) in enumerate(((lengths_in, lengths), (tiles_in, tiles), (flags_in, flags)))
    ]
    for copy in scalar_copies:
        copy.start()

    barrier = pltpu.get_barrier_semaphore()
    for step in STEPS:
        for along in (along_x, along_y):
            pl.semaphore_signal(barrier, inc=1, device_id=along(step)[1], device_id_type=MESH)
    pl.semaphore_wait(barrier, 6)

    def send(src, dst, send_sem, recv_sem, device):
        pltpu.make_async_remote_copy(
            src_ref=src, dst_ref=dst, send_sem=send_sem, recv_sem=recv_sem,
            device_id=device, device_id_type=MESH,
        ).start()

    def keep(src, dst, _, recv_sem):
        pltpu.make_async_copy(src, dst, recv_sem).start()

    def wait(ref, sem):
        pltpu.make_async_copy(ref, ref, sem).wait()

    def at(start, size):
        return pl.ds(pl.multiple_of(start, size), size)

    rows_c = at(c * ROWS, ROWS)
    rows_x = at(x * ROWS, ROWS)
    rows_hi = at(hi * ROWS, ROWS)

    def kv_even(n):
        cols = at(n * PAIR, PAIR)
        return [
            (k_in.at[0, :, cols], ek.at[rows_c, :], s_kv.at[0], r_kv.at[0]),
            (v_in.at[0, :, cols], ev.at[rows_c, :], s_kv.at[1], r_kv.at[1]),
        ]

    def kv_odd(n):
        cols = at(n * PAIR, PAIR)
        return [
            (k_in.at[1, :, cols], ok.at[low, rows_c, :], s_kv.at[2], r_kv.at[2]),
            (v_in.at[1, :, cols], ov.at[low, rows_c, :], s_kv.at[3], r_kv.at[3]),
        ]

    def q_even(n, j):
        cols = at(n * QPAIR + j * E_WIDTH, E_WIDTH)
        return [
            (q_in.at[0, :, cols], eq[j].at[rows_x, :], s_eq.at[j], r_eq.at[j]),
            (g_in.at[0, :, cols], eg[j].at[rows_x, :], s_eg.at[j], r_eg.at[j]),
        ]

    def q_odd(n, j):
        cols = at(n * QPAIR + j * O_WIDTH, O_WIDTH)
        return [
            (q_in.at[1, :, cols], oq[j].at[low, rows_hi, :], s_oq.at[j], r_oq.at[j]),
            (g_in.at[1, :, cols], og[j].at[low, rows_hi, :], s_og.at[j], r_og.at[j]),
        ]

    def exchange(even=None, odd=None):
        for step in STEPS:
            if odd is not None:
                n, device = along_y(step)
                for item in odd(n):
                    send(*item, device)
            if even is not None:
                n, device = along_x(step)
                for item in even(n):
                    send(*item, device)
        for item in (odd(y) if odd is not None else []) + (even(x) if even is not None else []):
            keep(*item)

    exchange(kv_even, kv_odd)
    exchange(lambda n: q_even(n, 0), lambda n: q_odd(n, 0))

    for copy in scalar_copies:
        copy.wait()
    flag = jnp.where(flags[dp] == 1, 1, 0)
    lane = lax.broadcasted_iota(jnp.int32, (BLOCK, BLOCK), 1)
    sub = lax.broadcasted_iota(jnp.int32, (BLOCK, BLOCK), 0)

    def segment_ends(seq):
        ends = []
        total = lengths[0, seq]
        for d in range(1, 8):
            ends.append(total)
            total = total + lengths[d, seq]
        return ends

    def addend(ends, row, col, tile):
        row_doc = sum((row >= e).astype(jnp.int32) for e in ends)
        col_doc = sum((col >= e).astype(jnp.int32) for e in ends)
        allowed = (col <= row) & ((col_doc == row_doc) | (col_doc == 0)) & (tile == 1)
        return jnp.where(allowed, 0.0, -1e30)

    wait(ok.at[:, 0 : 2 * ROWS, :], r_kv.at[2])
    wait(ov.at[:, 0 : 2 * ROWS, :], r_kv.at[3])
    for step in STEPS:
        _, device = along_x(step)
        for t in range(2):
            part = at((SIDE * t + x) * ROWS, ROWS)
            for n, ref in enumerate((ok, ov)):
                send(ref.at[:, part, :], ref.at[:, part, :], s_all.at[n], r_all.at[n], device)
    wait(ek.at[0 : SIDE * ROWS, :], r_kv.at[0])
    wait(ev.at[0 : SIDE * ROWS, :], r_kv.at[1])

    first = pl.ds(0, SIDE * ROWS)

    @pl.when(hi == 0)
    def _():
        for n, ref in enumerate((ek, ev)):
            send(ref.at[first, :], ref.at[first, :], s_fwd.at[n], r_fwd.at[n], across(1))

    for j in range(1, E_CHUNKS):
        odd = (lambda n, j=j: q_odd(n, j)) if j < O_CHUNKS else None
        exchange(lambda n, j=j: q_even(n, j), odd)

    for b in range(4):

        @pl.when(hi == b // 2)
        def _(b=b):
            seq = 2 * dp
            ends = segment_ends(seq)
            row = lane + BLOCK * b
            for n, cb in enumerate(COLUMN_BLOCKS[b]):
                top, bottom = (
                    jnp.where(
                        lane < 64,
                        tiles[2 * b, 2 * cb + m, seq],
                        tiles[2 * b + 1, 2 * cb + m, seq],
                    )
                    for m in range(2)
                )
                start = BIAS_START[b] + BLOCK * n
                ebias[start : start + BLOCK, :] = addend(
                    ends, row, sub + BLOCK * cb, jnp.where(sub < 64, top, bottom)
                )

    def source(slot):
        return slot + flag - 2 * slot * flag

    near = x + 2

    @pl.loop(0, 2)
    def _(slot):
        seq = 2 * (source(slot) * half + zc) + 1
        ends = segment_ends(seq)
        inner = lane % ROWS
        for t, start in ((0, 0), (0, BLOCK), (1, 2 * BLOCK)):
            row_tile = SIDE * t + x
            cb = start // BLOCK % 2
            tile = jnp.where(sub < 64, tiles[row_tile, 2 * cb, seq], tiles[row_tile, 2 * cb + 1, seq])
            obias[slot, start : start + BLOCK, :] = addend(
                ends, inner + row_tile * ROWS, sub + BLOCK * cb, tile
            )
        for m in range(3):
            start = 3 * BLOCK + ROWS * m
            tile = jnp.zeros_like(sub[:ROWS]) + tiles[SIDE + x, near + m, seq]
            obias[slot, start : start + ROWS, :] = addend(
                ends, inner[:ROWS] + (SIDE + x) * ROWS, sub[:ROWS] + (near + m) * ROWS, tile
            )

    for ref in (edk, edv, odk, odv):
        ref[...] = jnp.zeros_like(ref)

    def a_even(n, j):
        rows, cols = at(n * ROWS, ROWS), at(x * QPAIR + j * E_WIDTH, E_WIDTH)
        return [
            (ea.at[j, rows, :], attn_out.at[0, :, cols], s_ea.at[j], r_out.at[0]),
            (egq.at[j, rows, :], gq_out.at[0, :, cols], s_egq.at[j], r_out.at[1]),
        ]

    def a_odd(n, j):
        rows, cols = at((n // 2) * ROWS, ROWS), at(y * QPAIR + j * O_WIDTH, O_WIDTH)
        return [
            (oa.at[j, n % 2, rows, :], attn_out.at[1, :, cols], s_oa.at[j], r_out.at[0]),
            (ogq.at[j, n % 2, rows, :], gq_out.at[1, :, cols], s_ogq.at[j], r_out.at[1]),
        ]

    def kv_even_out(n):
        rows, cols = at(n * ROWS, ROWS), at(x * PAIR, PAIR)
        return [
            (egk.at[rows, :], gk_out.at[0, :, cols], s_gkv.at[0], r_out.at[2]),
            (egv.at[rows, :], gv_out.at[0, :, cols], s_gkv.at[1], r_out.at[3]),
        ]

    def kv_odd_out(n):
        cols = at(y * PAIR, PAIR)
        return [
            (ogk.at[n % 2, n // 2], gk_out.at[1, :, cols], s_gkv.at[2], r_out.at[2]),
            (ogv.at[n % 2, n // 2], gv_out.at[1, :, cols], s_gkv.at[3], r_out.at[3]),
        ]

    late = pl.ds(pl.multiple_of(near * ROWS, ROWS), 3 * ROWS)
    wait(ok.at[:, 0 : 6 * ROWS, :], r_all.at[0])
    wait(ov.at[:, 0 : 6 * ROWS, :], r_all.at[1])

    for j in range(O_CHUNKS):
        wait(oq[j], r_oq.at[j])
        wait(og[j], r_og.at[j])
        kv = slice(HEAD * j, HEAD * (j + 1))
        heads = [slice(HEAD * h, HEAD * (h + 1)) for h in range(RATIO)]

        @pl.loop(0, 2)
        def _(slot, j=j, kv=kv, heads=heads):
            u = source(slot)
            for t in range(2):
                rows = slice(ROWS * t, ROWS * (t + 1))
                queries = jnp.concatenate([oq[j][u, rows, h] for h in heads], axis=0)
                grads = jnp.concatenate([og[j][u, rows, h] for h in heads], axis=0)
                if t == 0:
                    keys, values = ok[u, 0:256, kv], ov[u, 0:256, kv]
                    mask = obias[slot, 0:256, :]
                else:
                    keys = jnp.concatenate([ok[u, 0:128, kv], ok[u, late, kv]], axis=0)
                    values = jnp.concatenate([ov[u, 0:128, kv], ov[u, late, kv]], axis=0)
                    mask = obias[slot, 256:576, :]
                attn, gq, dkp, dvp = attend(
                    queries, grads, keys, values, jnp.concatenate([mask] * 2, axis=1)
                )
                for n, h in enumerate(heads):
                    oa[j, slot, rows, h] = attn[ROWS * n : ROWS * (n + 1)]
                    ogq[j, slot, rows, h] = gq[ROWS * n : ROWS * (n + 1)]
                for ref, value in ((odk, dkp), (odv, dvp)):
                    if t == 0:
                        ref[slot, 0:256, kv] += value
                    else:
                        ref[slot, 0:128, kv] += value[:128]
                        ref[slot, late, kv] += value[128:]

        exchange(None, lambda n, j=j: a_odd(n, j))

    for t in range(8):
        rows = slice(ROWS * t, ROWS * (t + 1))
        opk[t % SIDE, :, t // SIDE] = (odk[:, rows] * SCALE).astype(jnp.bfloat16)
        opv[t % SIDE, :, t // SIDE] = odv[:, rows].astype(jnp.bfloat16)
    for step in STEPS:
        n, device = along_x(step)
        send(opk.at[n], rpk.at[step - 1], s_rs.at[0], r_rs.at[0], device)
        send(opv.at[n], rpv.at[step - 1], s_rs.at[1], r_rs.at[1], device)

    @pl.when(hi == 1)
    def _():
        wait(ek.at[first, :], r_fwd.at[0])
        wait(ev.at[first, :], r_fwd.at[1])

    for j in range(E_CHUNKS):
        wait(eq[j], r_eq.at[j])
        wait(eg[j], r_eg.at[j])
        g = j // 2
        kv = slice(HEAD * g, HEAD * (g + 1))
        heads = [slice(0, HEAD), slice(HEAD, 2 * HEAD)]
        for b in range(4):

            @pl.when(hi == b // 2)
            def _(b=b, j=j, kv=kv, heads=heads):
                blocks = COLUMN_BLOCKS[b]
                rows = slice(BLOCK * (b % 2), BLOCK * (b % 2 + 1))
                queries = jnp.concatenate([eq[j][rows, h] for h in heads], axis=0)
                grads = jnp.concatenate([eg[j][rows, h] for h in heads], axis=0)
                keys = jnp.concatenate([ek[BLOCK * n : BLOCK * (n + 1), kv] for n in blocks], axis=0)
                values = jnp.concatenate([ev[BLOCK * n : BLOCK * (n + 1), kv] for n in blocks], axis=0)
                mask = ebias[BIAS_START[b] : BIAS_START[b] + BLOCK * len(blocks), :]
                attn, gq, dkp, dvp = attend(
                    queries, grads, keys, values, jnp.concatenate([mask] * 2, axis=1)
                )
                for n, h in enumerate(heads):
                    ea[j, rows, h] = attn[BLOCK * n : BLOCK * (n + 1)]
                    egq[j, rows, h] = gq[BLOCK * n : BLOCK * (n + 1)]
                for ref, value in ((edk, dkp), (edv, dvp)):
                    for n, cb in enumerate(blocks):
                        ref[BLOCK * cb : BLOCK * (cb + 1), kv] += value[BLOCK * n : BLOCK * (n + 1)]

        if j % 2 == 1:

            @pl.when(hi == 1)
            def _(g=g, kv=kv):
                esk[g] = (edk[0:256, kv] * SCALE).astype(jnp.bfloat16)
                esv[g] = edv[0:256, kv].astype(jnp.bfloat16)
                send(esk.at[g], erk.at[g], s_ep.at[0, g], r_ep.at[0, g], across(0))
                send(esv.at[g], erv.at[g], s_ep.at[1, g], r_ep.at[1, g], across(0))

        exchange(lambda n, j=j: a_even(n, j))

        if j == 1:
            wait(rpk, r_rs.at[0])
            wait(rpv, r_rs.at[1])
            for t in range(2):
                rows = at((SIDE * t + x) * ROWS, ROWS)
                others = [ref[n, :, t].astype(jnp.float32) for ref in (rpk, rpv) for n in range(3)]
                ogk[:, t] = (odk[:, rows, :] * SCALE + others[0] + others[1] + others[2]).astype(
                    jnp.bfloat16
                )
                ogv[:, t] = (odv[:, rows, :] + others[3] + others[4] + others[5]).astype(jnp.bfloat16)
            exchange(None, kv_odd_out)

    @pl.when(hi == 0)
    def _():
        for g in range(2):
            kv = slice(HEAD * g, HEAD * (g + 1))
            wait(erk.at[g], r_ep.at[0, g])
            wait(erv.at[g], r_ep.at[1, g])
            egk[:, kv] = (edk[0:256, kv] * SCALE + erk[g].astype(jnp.float32)).astype(jnp.bfloat16)
            egv[:, kv] = (edv[0:256, kv] + erv[g].astype(jnp.float32)).astype(jnp.bfloat16)

    @pl.when(hi == 1)
    def _():
        egk[...] = (edk[256:512] * SCALE).astype(jnp.bfloat16)
        egv[...] = edv[256:512].astype(jnp.bfloat16)

    exchange(kv_even_out)

    three = 3 * ROWS
    for j in range(E_CHUNKS):
        wait(eq[j].at[0:three, :], s_eq.at[j])
        wait(eg[j].at[0:three, :], s_eg.at[j])
        wait(ea.at[j, 0:three, :], s_ea.at[j])
        wait(egq.at[j, 0:three, :], s_egq.at[j])
    for j in range(O_CHUNKS):
        wait(oq[j].at[:, 0 : three // 2, :], s_oq.at[j])
        wait(og[j].at[:, 0 : three // 2, :], s_og.at[j])
        wait(oa.at[j, :, 0 : three // 2, :], s_oa.at[j])
        wait(ogq.at[j, :, 0 : three // 2, :], s_ogq.at[j])
    for n in range(4):
        wait(ek.at[0:three, :], s_kv.at[n])
        wait(ek.at[0:three, :], s_gkv.at[n])
    for n in range(2):
        wait(ok.at[:, 0 : 2 * three, :], s_all.at[n])
        wait(opk.at[0:3], s_rs.at[n])

    @pl.when(hi == 0)
    def _():
        for n in range(2):
            wait(ek.at[first, :], s_fwd.at[n])

    @pl.when(hi == 1)
    def _():
        for n in range(2):
            for g in range(2):
                wait(esk.at[g], s_ep.at[n, g])

    for n, ref in enumerate((attn_out, gq_out, gk_out, gv_out)):
        wait(ref, r_out.at[n])


def finish_kernel(*refs):
    ins, outs, sem = refs[:4], refs[4:8], refs[8]
    for n in range(4):
        pltpu.make_async_copy(ins[n], outs[n], sem.at[n]).start()
    for n in range(4):
        pltpu.make_async_copy(ins[n], outs[n], sem.at[n]).wait()


def finish(arrays):
    anywhere = pl.BlockSpec(memory_space=pl.ANY)
    return pl.pallas_call(
        finish_kernel,
        out_shape=tuple(jax.ShapeDtypeStruct(a.shape, a.dtype) for a in arrays),
        in_specs=[anywhere] * 4,
        out_specs=(anywhere,) * 4,
        scratch_shapes=[pltpu.SemaphoreType.DMA((4,))],
    )(*[pltpu.with_memory_space_constraint(x, pltpu.VMEM) for x in arrays])


def shards(query_proj, key_proj, value_proj, grad_attn, doc_lengths, mask_tiles, pair_flags):
    bf16, f32 = jnp.bfloat16, jnp.float32
    dma, vmem = pltpu.SemaphoreType.DMA, pltpu.VMEM
    anywhere = pl.BlockSpec(memory_space=pl.ANY)
    scalars = (doc_lengths.T, jnp.transpose(mask_tiles, (1, 2, 0)), pair_flags)
    rows = SIDE * ROWS
    even_kv, odd_kv = vmem((LENGTH, PAIR), bf16), vmem((2, LENGTH, PAIR), bf16)
    even_a = vmem((E_CHUNKS, rows, E_WIDTH), bf16)
    odd_a = vmem((O_CHUNKS, 2, 2 * ROWS, O_WIDTH), bf16)
    even_d, odd_d = vmem((LENGTH, PAIR), f32), vmem((2, LENGTH, PAIR), f32)
    even_part, even_g = vmem((2, rows, HEAD), bf16), vmem((rows, PAIR), bf16)
    odd_part, odd_recv = vmem((4, 2, 2, ROWS, PAIR), bf16), vmem((3, 2, 2, ROWS, PAIR), bf16)
    odd_g = vmem((2, 2, ROWS, PAIR), bf16)
    return finish(pl.pallas_call(
        kernel,
        out_shape=tuple(
            jax.ShapeDtypeStruct(a.shape, bf16)
            for a in (query_proj, query_proj, key_proj, value_proj)
        ),
        in_specs=[anywhere] * 7,
        out_specs=(anywhere,) * 4,
        scratch_shapes=[
            even_kv, even_kv, odd_kv, odd_kv, even_a, even_a, odd_a, odd_a,
            even_d, even_d, odd_d, odd_d,
            vmem((6 * BLOCK, BLOCK), f32), vmem((2, 576, BLOCK), f32),
            even_part, even_part, even_part, even_part, even_g, even_g,
            odd_part, odd_part, odd_recv, odd_recv, odd_g, odd_g,
            *[pltpu.SMEM(a.shape, a.dtype) for a in scalars], dma((3,)),
            dma((E_CHUNKS,)), dma((E_CHUNKS,)), dma((O_CHUNKS,)), dma((O_CHUNKS,)),
            dma((4,)), dma((2,)), dma((2,)), dma((2, 2)), dma((2,)), dma((4,)),
            dma((E_CHUNKS,)), dma((E_CHUNKS,)), dma((O_CHUNKS,)), dma((O_CHUNKS,)),
            dma((4,)), dma((2,)), dma((2,)), dma((2, 2)), dma((2,)),
            dma((E_CHUNKS,)), dma((E_CHUNKS,)), dma((O_CHUNKS,)), dma((O_CHUNKS,)), dma((4,)),
            *[vmem((rows, E_WIDTH), bf16)] * (2 * E_CHUNKS),
            *[vmem((2, 2 * ROWS, O_WIDTH), bf16)] * (2 * O_CHUNKS),
        ],
        compiler_params=pltpu.CompilerParams(
            collective_id=0, has_side_effects=True, vmem_limit_bytes=48 * 2**20
        ),
    )(*[
        pltpu.with_memory_space_constraint(x, pltpu.HBM)
        for x in (query_proj, key_proj, value_proj, grad_attn, *scalars)
    ]))


def solution(mesh):
    split = P("dp", "ctx", None)
    return jax.shard_map(
        shards,
        mesh=mesh,
        in_specs=(split,) * 4 + (P(),) * 3,
        out_specs=(split,) * 4,
        check_vma=False,
    )
```

time: 66.6 us -> 61.9 us (0.929)
  Pallas kernels: 65.8 us -> 61.1 us
    pallas_call x1, Pallas kernels: 64.3 us -> 59.6 us  [shards(): pl.pallas_call(kernel, out_shape=tuple((jax.ShapeDtypeStruct(a.shape, bf1...]
where the time goes in v5:
time: 61.9 us; the launch traced here: 61.7 us
  Pallas kernels  61.1 us (99%)
  between operations  0.64 us (1%)
    pallas_call x1, Pallas kernels, shards(): pl.pallas_call(kernel, out_shape=tuple((jax.ShapeDtypeStruct(a.shape, bf1...  59.6 us
    pallas_call x1, Pallas kernels, finish(): pl.pallas_call(finish_kernel, out_shape=tuple((jax.ShapeDtypeStruct(a.sha...  1.52 us

profile of v5, /device:TPU:64, one launch (start us, length us, event | category | flops | bytes accessed | tf_op | source)
XLA Modules:
  0.0 61.7 jit_solution(14904741292654097410)
XLA Ops:
  0.6 59.6 %shard_map.102 = (bf16[2,64,4096]{2,1,0:T(8,128)(2,1)S(1)}, bf16[2,64,4096]{2,1,0:T(8,128)(2,1)S(1)}, bf16[2,64,1024]{2,1,0:T(8,128)(2,1)S(1)}, bf16[2,64,1024]{2,1,0:T(8,128)(2,1)S(1)}) custom-call(bf16[2,64,4096]{2,1,0:T(8,128)(2,1)} %q_in.1, bf16[2,64,1024]{2,1,0:T(8,128)(2,1)} %k_in.1, bf16[2,64,1024]{2,1,0:T(8,128)(2,1)} %v_in.1, ...), custom_call_target="tpu_custom_call" | custom-call | tf_op jit(solution)/shard_map/pallas_call | solution.py:463
  60.2 1.5 %shard_map.103 = (bf16[2,64,4096]{2,1,0:T(8,128)(2,1)}, bf16[2,64,4096]{2,1,0:T(8,128)(2,1)}, bf16[2,64,1024]{2,1,0:T(8,128)(2,1)}, bf16[2,64,1024]{2,1,0:T(8,128)(2,1)}) custom-call(bf16[2,64,4096]{2,1,0:T(8,128)(2,1)S(1)} %get-tuple-element.8.refs_0_, bf16[2,64,4096]{2,1,0:T(8,128)(2,1)S(1)} %get-tuple-element.9.refs_1_, ...), custom_call_target="tpu_custom_call" | custom-call | tf_op jit(solution)/shard_map/pallas_call | solution.py:441

commit v6 on v5

--- a/solution.py
+++ b/solution.py
@@ -53,9 +53,9 @@
     q_in, k_in, v_in, g_in, lengths_in, tiles_in, flags_in,
     attn_out, gq_out, gk_out, gv_out,
     ek, ev, ok, ov, ea, egq, oa, ogq, edk, edv, odk, odv, ebias, obias,
-    esk, esv, erk, erv, egk, egv, opk, opv, rpk, rpv, ogk, ogv,
+    esk, esv, erk, erv, egk, egv, opk, opv, rpk, rpv, ogk, ogv, rtk, rtv, ctk, ctv, r_rt, s_ct,
     lengths, tiles, flags, scalar_sem,
-    r_eq, r_eg, r_oq, r_og, r_kv, r_all, r_fwd, r_ep, r_rs, r_out,
+    r_eq, r_eg, r_oq, r_og, r_kv, r_all, r_fwd, r_ep, r_rs, r_out, r_rel, s_rel,
     s_eq, s_eg, s_oq, s_og, s_kv, s_all, s_fwd, s_ep, s_rs,
     s_ea, s_egq, s_oa, s_ogq, s_gkv,
     *bufs,
@@ -180,12 +180,13 @@
 
     wait(ok.at[:, 0 : 2 * ROWS, :], r_kv.at[2])
     wait(ov.at[:, 0 : 2 * ROWS, :], r_kv.at[3])
-    for step in STEPS:
+    for side, step in enumerate((1, 3)):
         _, device = along_x(step)
         for t in range(2):
             part = at((SIDE * t + x) * ROWS, ROWS)
             for n, ref in enumerate((ok, ov)):
-                send(ref.at[:, part, :], ref.at[:, part, :], s_all.at[n], r_all.at[n], device)
+                here = ref.at[:, part, :]
+                send(here, here, s_all.at[n], r_all.at[2 * side + n], device)
     wait(ek.at[0 : SIDE * ROWS, :], r_kv.at[0])
     wait(ev.at[0 : SIDE * ROWS, :], r_kv.at[1])
 
@@ -196,9 +197,7 @@
         for n, ref in enumerate((ek, ev)):
             send(ref.at[first, :], ref.at[first, :], s_fwd.at[n], r_fwd.at[n], across(1))
 
-    for j in range(1, E_CHUNKS):
-        odd = (lambda n, j=j: q_odd(n, j)) if j < O_CHUNKS else None
-        exchange(lambda n, j=j: q_even(n, j), odd)
+    exchange(lambda n: q_even(n, 1), lambda n: q_odd(n, 1))
 
     for b in range(4):
 
@@ -221,6 +220,18 @@
                     ends, row, sub + BLOCK * cb, jnp.where(sub < 64, top, bottom)
                 )
 
+    for side, step in enumerate((1, 3)):
+        _, device = along_x(step)
+        for n, ref in enumerate((ok, ov)):
+            wait(ref.at[:, 0 : 2 * ROWS, :], r_all.at[2 * side + n])
+            for t in range(2):
+                part = at((SIDE * t + (x + 4 - step) % SIDE) * ROWS, ROWS)
+                here = ref.at[side, part, :]
+                send(here, here, s_rel.at[n], r_rel.at[2 * side + n], device)
+
+    for j in range(2, E_CHUNKS):
+        exchange(lambda n, j=j: q_even(n, j))
+
     def source(slot):
         return slot + flag - 2 * slot * flag
 
@@ -277,8 +288,9 @@
         ]
 
     late = pl.ds(pl.multiple_of(near * ROWS, ROWS), 3 * ROWS)
-    wait(ok.at[:, 0 : 6 * ROWS, :], r_all.at[0])
-    wait(ov.at[:, 0 : 6 * ROWS, :], r_all.at[1])
+    for side in range(2):
+        for n, ref in enumerate((ok, ov)):
+            wait(ref.at[side, 0 : 2 * ROWS, :], r_rel.at[2 * side + n])
 
     for j in range(O_CHUNKS):
         wait(oq[j], r_oq.at[j])
@@ -319,10 +331,12 @@
         rows = slice(ROWS * t, ROWS * (t + 1))
         opk[t % SIDE, :, t // SIDE] = (odk[:, rows] * SCALE).astype(jnp.bfloat16)
         opv[t % SIDE, :, t // SIDE] = odv[:, rows].astype(jnp.bfloat16)
-    for step in STEPS:
-        n, device = along_x(step)
-        send(opk.at[n], rpk.at[step - 1], s_rs.at[0], r_rs.at[0], device)
-        send(opv.at[n], rpv.at[step - 1], s_rs.at[1], r_rs.at[1], device)
+    far = (x + 2) % SIDE
+    for n, (op, rt, rp) in enumerate(((opk, rtk, rpk), (opv, rtv, rpv))):
+        for side, step in enumerate((1, 3)):
+            near_x, device = along_x(step)
+            send(op.at[far, side], rt.at[side], s_rs.at[n], r_rt.at[n], device)
+            send(op.at[near_x, 1 - side], rp.at[side, 1 - side], s_rs.at[n], r_rs.at[n], device)
 
     @pl.when(hi == 1)
     def _():
@@ -367,16 +381,30 @@
 
         exchange(lambda n, j=j: a_even(n, j))
 
-        if j == 1:
+        if j == 0:
+            for n, (ref, rt, ct, rp, scale) in enumerate(
+                ((odk, rtk, ctk, rpk, SCALE), (odv, rtv, ctv, rpv, 1.0))
+            ):
+                wait(rt, r_rt.at[n])
+                for side, step in enumerate((1, 3)):
+                    near_x, device = along_x(step)
+                    for t in range(2):
+                        rows = at((SIDE * t + near_x) * ROWS, ROWS)
+                        ct[side, t] = (
+                            ref[side, rows, :] * scale + rt[side, t].astype(jnp.float32)
+                        ).astype(jnp.bfloat16)
+                    send(ct.at[side], rp.at[side, side], s_ct.at[n], r_rs.at[n], device)
+
+        if j == 2:
             wait(rpk, r_rs.at[0])
             wait(rpv, r_rs.at[1])
             for t in range(2):
                 rows = at((SIDE * t + x) * ROWS, ROWS)
-                others = [ref[n, :, t].astype(jnp.float32) for ref in (rpk, rpv) for n in range(3)]
-                ogk[:, t] = (odk[:, rows, :] * SCALE + others[0] + others[1] + others[2]).astype(
+                others = [ref[n, :, t].astype(jnp.float32) for ref in (rpk, rpv) for n in range(2)]
+                ogk[:, t] = (odk[:, rows, :] * SCALE + others[0] + others[1]).astype(
                     jnp.bfloat16
                 )
-                ogv[:, t] = (odv[:, rows, :] + others[3] + others[4] + others[5]).astype(jnp.bfloat16)
+                ogv[:, t] = (odv[:, rows, :] + others[2] + others[3]).astype(jnp.bfloat16)
             exchange(None, kv_odd_out)
 
     @pl.when(hi == 0)
@@ -410,8 +438,10 @@
         wait(ek.at[0:three, :], s_kv.at[n])
         wait(ek.at[0:three, :], s_gkv.at[n])
     for n in range(2):
-        wait(ok.at[:, 0 : 2 * three, :], s_all.at[n])
-        wait(opk.at[0:3], s_rs.at[n])
+        wait(ok.at[:, 0 : 4 * ROWS, :], s_all.at[n])
+        wait(ok.at[:, 0 : 2 * ROWS, :], s_rel.at[n])
+        wait(opk.at[0:2], s_rs.at[n])
+        wait(ctk, s_ct.at[n])
 
     @pl.when(hi == 0)
     def _():
@@ -458,7 +488,7 @@
     odd_a = vmem((O_CHUNKS, 2, 2 * ROWS, O_WIDTH), bf16)
     even_d, odd_d = vmem((LENGTH, PAIR), f32), vmem((2, LENGTH, PAIR), f32)
     even_part, even_g = vmem((2, rows, HEAD), bf16), vmem((rows, PAIR), bf16)
-    odd_part, odd_recv = vmem((4, 2, 2, ROWS, PAIR), bf16), vmem((3, 2, 2, ROWS, PAIR), bf16)
+    odd_part, odd_recv = vmem((4, 2, 2, ROWS, PAIR), bf16), vmem((2, 2, 2, ROWS, PAIR), bf16)
     odd_g = vmem((2, 2, ROWS, PAIR), bf16)
     return finish(pl.pallas_call(
         kernel,
@@ -474,9 +504,10 @@
             vmem((6 * BLOCK, BLOCK), f32), vmem((2, 576, BLOCK), f32),
             even_part, even_part, even_part, even_part, even_g, even_g,
             odd_part, odd_part, odd_recv, odd_recv, odd_g, odd_g,
+            odd_g, odd_g, odd_g, odd_g, dma((2,)), dma((2,)),
             *[pltpu.SMEM(a.shape, a.dtype) for a in scalars], dma((3,)),
             dma((E_CHUNKS,)), dma((E_CHUNKS,)), dma((O_CHUNKS,)), dma((O_CHUNKS,)),
-            dma((4,)), dma((2,)), dma((2,)), dma((2, 2)), dma((2,)), dma((4,)),
+            dma((4,)), dma((4,)), dma((2,)), dma((2, 2)), dma((2,)), dma((4,)), dma((4,)), dma((2,)),
             dma((E_CHUNKS,)), dma((E_CHUNKS,)), dma((O_CHUNKS,)), dma((O_CHUNKS,)),
             dma((4,)), dma((2,)), dma((2,)), dma((2, 2)), dma((2,)),
             dma((E_CHUNKS,)), dma((E_CHUNKS,)), dma((O_CHUNKS,)), dma((O_CHUNKS,)), dma((4,)),

time: 61.9 us -> 59.8 us (0.966)
  Pallas kernels: 61.1 us -> 59 us
    pallas_call x1, Pallas kernels: 59.6 us -> 57.5 us  [shards(): pl.pallas_call(kernel, out_shape=tuple((jax.ShapeDtypeStruct(a.shape, bf1...]
where the time goes in v6:
time: 59.8 us; the launch traced here: 59.7 us
  Pallas kernels  59 us (99%)
  between operations  0.64 us (1%)
    pallas_call x1, Pallas kernels, shards(): pl.pallas_call(kernel, out_shape=tuple((jax.ShapeDtypeStruct(a.shape, bf1...  57.5 us
    pallas_call x1, Pallas kernels, finish(): pl.pallas_call(finish_kernel, out_shape=tuple((jax.ShapeDtypeStruct(a.sha...  1.52 us

profile of v6, /device:TPU:64, one launch (start us, length us, event | category | flops | bytes accessed | tf_op | source)
XLA Modules:
  0.0 59.7 jit_solution(1073612220763298108)
XLA Ops:
  0.6 57.5 %shard_map.102 = (bf16[2,64,4096]{2,1,0:T(8,128)(2,1)S(1)}, bf16[2,64,4096]{2,1,0:T(8,128)(2,1)S(1)}, bf16[2,64,1024]{2,1,0:T(8,128)(2,1)S(1)}, bf16[2,64,1024]{2,1,0:T(8,128)(2,1)S(1)}) custom-call(bf16[2,64,4096]{2,1,0:T(8,128)(2,1)} %q_in.1, bf16[2,64,1024]{2,1,0:T(8,128)(2,1)} %k_in.1, bf16[2,64,1024]{2,1,0:T(8,128)(2,1)} %v_in.1, ...), custom_call_target="tpu_custom_call" | custom-call | tf_op jit(solution)/shard_map/pallas_call | solution.py:493
  58.1 1.5 %shard_map.103 = (bf16[2,64,4096]{2,1,0:T(8,128)(2,1)}, bf16[2,64,4096]{2,1,0:T(8,128)(2,1)}, bf16[2,64,1024]{2,1,0:T(8,128)(2,1)}, bf16[2,64,1024]{2,1,0:T(8,128)(2,1)}) custom-call(bf16[2,64,4096]{2,1,0:T(8,128)(2,1)S(1)} %get-tuple-element.8.refs_0_, bf16[2,64,4096]{2,1,0:T(8,128)(2,1)S(1)} %get-tuple-element.9.refs_1_, ...), custom_call_target="tpu_custom_call" | custom-call | tf_op jit(solution)/shard_map/pallas_call | solution.py:471

commit v7 on v6

--- a/solution.py
+++ b/solution.py
@@ -288,11 +288,12 @@
         ]
 
     late = pl.ds(pl.multiple_of(near * ROWS, ROWS), 3 * ROWS)
-    for side in range(2):
-        for n, ref in enumerate((ok, ov)):
-            wait(ref.at[side, 0 : 2 * ROWS, :], r_rel.at[2 * side + n])
-
-    for j in range(O_CHUNKS):
+    def odd_ready():
+        for side in range(2):
+            for n, ref in enumerate((ok, ov)):
+                wait(ref.at[side, 0 : 2 * ROWS, :], r_rel.at[2 * side + n])
+
+    def odd_chunk(j):
         wait(oq[j], r_oq.at[j])
         wait(og[j], r_og.at[j])
         kv = slice(HEAD * j, HEAD * (j + 1))
@@ -327,23 +328,25 @@
 
         exchange(None, lambda n, j=j: a_odd(n, j))
 
-    for t in range(8):
-        rows = slice(ROWS * t, ROWS * (t + 1))
-        opk[t % SIDE, :, t // SIDE] = (odk[:, rows] * SCALE).astype(jnp.bfloat16)
-        opv[t % SIDE, :, t // SIDE] = odv[:, rows].astype(jnp.bfloat16)
-    far = (x + 2) % SIDE
-    for n, (op, rt, rp) in enumerate(((opk, rtk, rpk), (opv, rtv, rpv))):
-        for side, step in enumerate((1, 3)):
-            near_x, device = along_x(step)
-            send(op.at[far, side], rt.at[side], s_rs.at[n], r_rt.at[n], device)
-            send(op.at[near_x, 1 - side], rp.at[side, 1 - side], s_rs.at[n], r_rs.at[n], device)
-
-    @pl.when(hi == 1)
-    def _():
-        wait(ek.at[first, :], r_fwd.at[0])
-        wait(ev.at[first, :], r_fwd.at[1])
-
-    for j in range(E_CHUNKS):
+    def odd_partials():
+        for t in range(8):
+            rows = slice(ROWS * t, ROWS * (t + 1))
+            opk[t % SIDE, :, t // SIDE] = (odk[:, rows] * SCALE).astype(jnp.bfloat16)
+            opv[t % SIDE, :, t // SIDE] = odv[:, rows].astype(jnp.bfloat16)
+        far = (x + 2) % SIDE
+        for n, (op, rt, rp) in enumerate(((opk, rtk, rpk), (opv, rtv, rpv))):
+            for side, step in enumerate((1, 3)):
+                near_x, device = along_x(step)
+                send(op.at[far, side], rt.at[side], s_rs.at[n], r_rt.at[n], device)
+                send(op.at[near_x, 1 - side], rp.at[side, 1 - side], s_rs.at[n], r_rs.at[n], device)
+
+    def even_ready():
+        @pl.when(hi == 1)
+        def _():
+            wait(ek.at[first, :], r_fwd.at[0])
+            wait(ev.at[first, :], r_fwd.at[1])
+
+    def even_chunk(j):
         wait(eq[j], r_eq.at[j])
         wait(eg[j], r_eg.at[j])
         g = j // 2
@@ -381,31 +384,43 @@
 
         exchange(lambda n, j=j: a_even(n, j))
 
-        if j == 0:
-            for n, (ref, rt, ct, rp, scale) in enumerate(
-                ((odk, rtk, ctk, rpk, SCALE), (odv, rtv, ctv, rpv, 1.0))
-            ):
-                wait(rt, r_rt.at[n])
-                for side, step in enumerate((1, 3)):
-                    near_x, device = along_x(step)
-                    for t in range(2):
-                        rows = at((SIDE * t + near_x) * ROWS, ROWS)
-                        ct[side, t] = (
-                            ref[side, rows, :] * scale + rt[side, t].astype(jnp.float32)
-                        ).astype(jnp.bfloat16)
-                    send(ct.at[side], rp.at[side, side], s_ct.at[n], r_rs.at[n], device)
-
-        if j == 2:
-            wait(rpk, r_rs.at[0])
-            wait(rpv, r_rs.at[1])
-            for t in range(2):
-                rows = at((SIDE * t + x) * ROWS, ROWS)
-                others = [ref[n, :, t].astype(jnp.float32) for ref in (rpk, rpv) for n in range(2)]
-                ogk[:, t] = (odk[:, rows, :] * SCALE + others[0] + others[1]).astype(
-                    jnp.bfloat16
-                )
-                ogv[:, t] = (odv[:, rows, :] + others[2] + others[3]).astype(jnp.bfloat16)
-            exchange(None, kv_odd_out)
+    def odd_relay():
+        for n, (ref, rt, ct, rp, scale) in enumerate(
+            ((odk, rtk, ctk, rpk, SCALE), (odv, rtv, ctv, rpv, 1.0))
+        ):
+            wait(rt, r_rt.at[n])
+            for side, step in enumerate((1, 3)):
+                near_x, device = along_x(step)
+                for t in range(2):
+                    rows = at((SIDE * t + near_x) * ROWS, ROWS)
+                    ct[side, t] = (
+                        ref[side, rows, :] * scale + rt[side, t].astype(jnp.float32)
+                    ).astype(jnp.bfloat16)
+                send(ct.at[side], rp.at[side, side], s_ct.at[n], r_rs.at[n], device)
+
+    def odd_final():
+        wait(rpk, r_rs.at[0])
+        wait(rpv, r_rs.at[1])
+        for t in range(2):
+            rows = at((SIDE * t + x) * ROWS, ROWS)
+            others = [ref[n, :, t].astype(jnp.float32) for ref in (rpk, rpv) for n in range(2)]
+            ogk[:, t] = (odk[:, rows, :] * SCALE + others[0] + others[1]).astype(
+                jnp.bfloat16
+            )
+            ogv[:, t] = (odv[:, rows, :] + others[2] + others[3]).astype(jnp.bfloat16)
+        exchange(None, kv_odd_out)
+
+    even_ready()
+    even_chunk(0)
+    even_chunk(1)
+    odd_ready()
+    odd_chunk(0)
+    odd_chunk(1)
+    odd_partials()
+    even_chunk(2)
+    odd_relay()
+    even_chunk(3)
+    odd_final()
 
     @pl.when(hi == 0)
     def _():

time: 59.8 us -> 56 us (0.936)
  Pallas kernels: 59 us -> 55.2 us
    pallas_call x1, Pallas kernels: 57.5 us -> 53.7 us  [shards(): pl.pallas_call(kernel, out_shape=tuple((jax.ShapeDtypeStruct(a.shape, bf1...]
where the time goes in v7:
time: 56 us; the launch traced here: 55.9 us
  Pallas kernels  55.2 us (99%)
  between operations  0.64 us (1%)
    pallas_call x1, Pallas kernels, shards(): pl.pallas_call(kernel, out_shape=tuple((jax.ShapeDtypeStruct(a.shape, bf1...  53.7 us
    pallas_call x1, Pallas kernels, finish(): pl.pallas_call(finish_kernel, out_shape=tuple((jax.ShapeDtypeStruct(a.sha...  1.52 us

profile of v7, /device:TPU:64, one launch (start us, length us, event | category | flops | bytes accessed | tf_op | source)
XLA Modules:
  0.0 55.9 jit_solution(16864561140580446870)
XLA Ops:
  0.6 53.7 %shard_map.102 = (bf16[2,64,4096]{2,1,0:T(8,128)(2,1)S(1)}, bf16[2,64,4096]{2,1,0:T(8,128)(2,1)S(1)}, bf16[2,64,1024]{2,1,0:T(8,128)(2,1)S(1)}, bf16[2,64,1024]{2,1,0:T(8,128)(2,1)S(1)}) custom-call(bf16[2,64,4096]{2,1,0:T(8,128)(2,1)} %q_in.1, bf16[2,64,1024]{2,1,0:T(8,128)(2,1)} %k_in.1, bf16[2,64,1024]{2,1,0:T(8,128)(2,1)} %v_in.1, ...), custom_call_target="tpu_custom_call" | custom-call | tf_op jit(solution)/shard_map/pallas_call | solution.py:508
  54.3 1.5 %shard_map.103 = (bf16[2,64,4096]{2,1,0:T(8,128)(2,1)}, bf16[2,64,4096]{2,1,0:T(8,128)(2,1)}, bf16[2,64,1024]{2,1,0:T(8,128)(2,1)}, bf16[2,64,1024]{2,1,0:T(8,128)(2,1)}) custom-call(bf16[2,64,4096]{2,1,0:T(8,128)(2,1)S(1)} %get-tuple-element.8.refs_0_, bf16[2,64,4096]{2,1,0:T(8,128)(2,1)S(1)} %get-tuple-element.9.refs_1_, ...), custom_call_target="tpu_custom_call" | custom-call | tf_op jit(solution)/shard_map/pallas_call | solution.py:486

commit v8 on v7

--- a/solution.py
+++ b/solution.py
@@ -156,7 +156,7 @@
             keep(*item)
 
     exchange(kv_even, kv_odd)
-    exchange(lambda n: q_even(n, 0), lambda n: q_odd(n, 0))
+    exchange(lambda n: q_even(n, 0))
 
     for copy in scalar_copies:
         copy.wait()
@@ -197,7 +197,7 @@
         for n, ref in enumerate((ek, ev)):
             send(ref.at[first, :], ref.at[first, :], s_fwd.at[n], r_fwd.at[n], across(1))
 
-    exchange(lambda n: q_even(n, 1), lambda n: q_odd(n, 1))
+    exchange(lambda n: q_even(n, 1), lambda n: q_odd(n, 0))
 
     for b in range(4):
 
@@ -229,8 +229,8 @@
                 here = ref.at[side, part, :]
                 send(here, here, s_rel.at[n], r_rel.at[2 * side + n], device)
 
-    for j in range(2, E_CHUNKS):
-        exchange(lambda n, j=j: q_even(n, j))
+    exchange(lambda n: q_even(n, 2), lambda n: q_odd(n, 1))
+    exchange(lambda n: q_even(n, 3))
 
     def source(slot):
         return slot + flag - 2 * slot * flag

time: 56 us -> 55.1 us (0.984)
  Pallas kernels: 55.2 us -> 54.3 us
    pallas_call x1, Pallas kernels: 53.7 us -> 52.8 us  [shards(): pl.pallas_call(kernel, out_shape=tuple((jax.ShapeDtypeStruct(a.shape, bf1...]
where the time goes in v8:
time: 55.1 us; the launch traced here: 55 us
  Pallas kernels  54.3 us (99%)
  between operations  0.64 us (1%)
    pallas_call x1, Pallas kernels, shards(): pl.pallas_call(kernel, out_shape=tuple((jax.ShapeDtypeStruct(a.shape, bf1...  52.8 us
    pallas_call x1, Pallas kernels, finish(): pl.pallas_call(finish_kernel, out_shape=tuple((jax.ShapeDtypeStruct(a.sha...  1.52 us

profile of v8, /device:TPU:64, one launch (start us, length us, event | category | flops | bytes accessed | tf_op | source)
XLA Modules:
  0.0 55.0 jit_solution(12645557364380757546)
XLA Ops:
  0.6 52.8 %shard_map.102 = (bf16[2,64,4096]{2,1,0:T(8,128)(2,1)S(1)}, bf16[2,64,4096]{2,1,0:T(8,128)(2,1)S(1)}, bf16[2,64,1024]{2,1,0:T(8,128)(2,1)S(1)}, bf16[2,64,1024]{2,1,0:T(8,128)(2,1)S(1)}) custom-call(bf16[2,64,4096]{2,1,0:T(8,128)(2,1)} %q_in.1, bf16[2,64,1024]{2,1,0:T(8,128)(2,1)} %k_in.1, bf16[2,64,1024]{2,1,0:T(8,128)(2,1)} %v_in.1, ...), custom_call_target="tpu_custom_call" | custom-call | tf_op jit(solution)/shard_map/pallas_call | solution.py:508
  53.4 1.5 %shard_map.103 = (bf16[2,64,4096]{2,1,0:T(8,128)(2,1)}, bf16[2,64,4096]{2,1,0:T(8,128)(2,1)}, bf16[2,64,1024]{2,1,0:T(8,128)(2,1)}, bf16[2,64,1024]{2,1,0:T(8,128)(2,1)}) custom-call(bf16[2,64,4096]{2,1,0:T(8,128)(2,1)S(1)} %get-tuple-element.8.refs_0_, bf16[2,64,4096]{2,1,0:T(8,128)(2,1)S(1)} %get-tuple-element.9.refs_1_, ...), custom_call_target="tpu_custom_call" | custom-call | tf_op jit(solution)/shard_map/pallas_call | solution.py:486
